TPU v7x, 256 devices: a whole 4x4x8 slice. The times are simulated.
256 devices in a mesh: doc: 16 (over z, y_lo), leaf: 16 (over x, y_hi, core).
Axes of the slice: x: 4, y: 4 (y_hi: 2, y_lo: 2; y = y_hi * 2 + y_lo), z: 8, core: 2. Of those that a mesh axis runs over, the one named last changes fastest.
Arguments:
- features: bfloat16 [262144, 256], P(('doc', 'leaf'))
- scores: float32 [262144], P(('doc', 'leaf')), may hold values from -6 to 6
- labels: int32 [262144], P(('doc', 'leaf')), may hold values from 0 to 4
- query_ids: int32 [262144], P(('doc', 'leaf')), may hold values from 0 to 8186, as said below
- ranks: int32 [262144], P(('doc', 'leaf')), may hold values from 1 to 128, as said below
- leaf_ids: int32 [262144], P(('doc', 'leaf')), may hold values from 0 to 15
Outputs:
- gradients: float32 [262144], P(('doc', 'leaf'))
- tree_output: float32 [262144], P(('doc', 'leaf'))
- new_scores: float32 [262144], P(('doc', 'leaf'))
Inputs may be any that keep to these rules, and one draw needn't show every extreme that they name: `query_ids`: the rows of one query are contiguous; ids are 0 on the first row and rise by one at each new query; a query has 1 to 128 rows and some query has exactly 128. Within each query the ranks of its rows are the numbers 1 to its row count, each once.
All inputs are finite; a program needn't handle non-finite values.
Results may differ from a plain program's by a relative error of at most 0.0038.
Values sent between devices are 32-bit elements; how exact they have to be, the bound alone decides.
A program may use at most 64 MiB of HBM per device.

v0:
```python
import math

import jax
import jax.numpy as jnp
from jax import lax
from jax.sharding import Mesh
from jax.sharding import PartitionSpec as P

LEAVES = 16
MAXQ = 128
DOC_LEAF = ("doc", "leaf_0", "leaf_1", "leaf_2")
LEAF = ("leaf_0", "leaf_1", "leaf_2")


LAMBDA = 1.0
SHRINKAGE = 0.1


def passed_along(value, axis, by):
    devices = lax.axis_size(axis)
    pairs = [(i, i + by) for i in range(devices) if 0 <= i + by < devices]
    return lax.ppermute(value, axis, pairs)


def in_blocks(value, dim, devices):
    lengths = value.shape
    pieces = value.reshape(*lengths[:dim], devices, lengths[dim] // devices, *lengths[dim + 1 :])
    return jnp.moveaxis(pieces, dim, 0)


def sent_and_summed(value, axis, dim):
    pieces = in_blocks(value, dim, lax.axis_size(axis))
    arrived = lax.all_to_all(pieces, axis, split_axis=0, concat_axis=0, tiled=True)
    return arrived.sum(axis=0)


def sum_in_two_steps(value, axes, dim):
    far, near = axes
    own = sent_and_summed(in_blocks(value, dim, lax.axis_size(far)), near, dim + 1)
    return jnp.sum(lax.all_to_all(own, far, 0, 0, tiled=True), axis=0)


def rows_for(lines, devices):
    spare = -len(lines) % devices
    return jnp.pad(lines, [(0, spare)] + [(0, 0)] * (lines.ndim - 1))


def in_order(pieces, dim):
    lengths = list(pieces.shape[1:])
    lengths[dim] *= pieces.shape[0]
    return jnp.moveaxis(pieces, 0, dim).reshape(lengths)


def from_everyone(value, axis):
    devices = lax.axis_size(axis)
    return lax.all_to_all(
        jnp.broadcast_to(value[None], (devices, *value.shape)), axis, 0, 0, tiled=True
    )


def collect(value, axis, dim):
    return in_order(from_everyone(value, axis), dim)


def total_of(value, axes):
    lines = value.reshape(-1)
    padded = rows_for(lines, lax.axis_size(axes))
    whole = collect(sent_and_summed(padded, axes, 0), axes, 0)
    return lax.slice_in_dim(whole, 0, len(lines)).reshape(value.shape)


def in_one_piece(arrays, axis, dim, along):
    widths = [math.prod(a.shape[along:]) for a in arrays]
    both = jnp.concatenate(
        [a.reshape(*a.shape[:along], w) for a, w in zip(arrays, widths)], axis=along
    )
    out = lax.all_gather(both, axis, axis=dim, tiled=True)
    pieces = jnp.split(out, [sum(widths[:k]) for k in range(1, len(widths))], axis=along)
    return tuple((b.reshape(*out.shape[:along], *a.shape[along:]) for a, b in zip(arrays, pieces)))


def discount(rank_values):
    return 1.0 / jnp.log2(1.0 + jnp.maximum(rank_values, 1.0))


def pair_block(own_rows, window):
    same_query = own_rows[0][:, None] == window[0][None, :]
    own_label = own_rows[1][:, None]
    far_label = window[1][None, :]
    counts = jnp.stack(
        [
            jnp.sum(jnp.where(same_query & (far_label >= grade_level), 1.0, 0.0), axis=1)
            for grade_level in (1.0, 2.0, 3.0, 4.0)
        ],
        axis=1,
    )
    positions = jnp.arange(1, MAXQ + 1).astype(jnp.float32)
    prefix = jnp.sum(
        jnp.where(
            positions[None, None, :] <= counts[:, :, None], discount(positions)[None, None, :], 0.0
        ),
        axis=2,
    )
    ideal_gain = jnp.sum(prefix * jnp.array([1.0, 2.0, 4.0, 8.0], jnp.float32)[None, :], axis=1)
    inverse = 1.0 / jnp.maximum(ideal_gain, 1.0)
    gain_gap = jnp.abs(jnp.exp2(own_label) - jnp.exp2(far_label))
    disc_gap = jnp.abs(discount(own_rows[2])[:, None] - discount(window[2])[None, :])
    direction = jnp.sign(own_label - far_label)
    weight = jnp.where(same_query, gain_gap * disc_gap, 0.0)
    pair_prob = jax.nn.sigmoid(-direction * (own_rows[3][:, None] - window[3][None, :]))
    gradient = -inverse * jnp.sum(direction * weight * pair_prob, axis=1)
    hessian = inverse * jnp.sum(weight * pair_prob * (1.0 - pair_prob), axis=1)
    return (gradient, hessian)


def solve_leaf(leaf_block):
    feature_count = leaf_block.shape[1]
    gram_matrix = leaf_block[:feature_count]
    weighted_sum = leaf_block[feature_count]
    moment = leaf_block[feature_count + 1]
    hess_total = leaf_block[feature_count + 2, 0]
    grad_total = leaf_block[feature_count + 2, 1]
    denominator = hess_total + LAMBDA
    system = (
        gram_matrix
        + LAMBDA * jnp.eye(feature_count, dtype=jnp.float32)
        - weighted_sum[:, None] * weighted_sum[None, :] / denominator
    )
    right_side = weighted_sum * grad_total / denominator - moment
    factor = jnp.linalg.cholesky(system)
    middle = lax.linalg.triangular_solve(factor, right_side[:, None], left_side=True, lower=True)
    coefficients = lax.linalg.triangular_solve(
        factor, middle, left_side=True, lower=True, transpose_a=True
    )[:, 0]
    intercept = -(grad_total + jnp.sum(weighted_sum * coefficients)) / denominator
    return (coefficients, intercept)


def body(features, scores, labels, query_ids, ranks, leaf_ids):
    row_count = features.shape[0]
    feature_count = features.shape[1]
    row_info = jnp.stack(
        [
            (query_ids + 1).astype(jnp.float32),
            labels.astype(jnp.float32),
            ranks.astype(jnp.float32),
            scores,
        ]
    )
    leading = passed_along(row_info[:, row_count - MAXQ :], DOC_LEAF, 1)
    trailing = passed_along(row_info[:, :MAXQ], DOC_LEAF, -1)
    padded = jnp.concatenate([leading, row_info, trailing], axis=1)
    block_rows = min(512, row_count)
    zero_index = jnp.zeros((), jnp.int32)

    def one_block(block_start):
        own_rows = lax.dynamic_slice(padded, (zero_index, block_start + MAXQ), (4, block_rows))
        window = lax.dynamic_slice(padded, (zero_index, block_start), (4, block_rows + 2 * MAXQ))
        return pair_block(own_rows, window)

    starts = jnp.arange(row_count // block_rows) * block_rows
    block_grads, block_hess = lax.map(one_block, starts)
    gradients = block_grads.reshape(-1)
    hessians = block_hess.reshape(-1)

    def leaf_terms(leaf_number):
        in_leaf = (leaf_ids == leaf_number).astype(jnp.float32)
        weighted = ((hessians * in_leaf)[:, None] * features).astype(jnp.bfloat16)
        gram_matrix = lax.dot_general(
            weighted, features, (((0,), (0,)), ((), ())), preferred_element_type=jnp.float32
        )
        weighted_sum = jnp.sum(weighted.astype(jnp.float32), axis=0)
        grad_low = (gradients * in_leaf).astype(jnp.bfloat16)
        moment = jnp.dot(grad_low, features, preferred_element_type=jnp.float32)
        total_rows = jnp.zeros((6, feature_count), jnp.float32)
        total_rows = (
            total_rows.at[0, 0]
            .set(jnp.sum(hessians * in_leaf))
            .at[0, 1]
            .set(jnp.sum(gradients * in_leaf))
        )
        return jnp.concatenate(
            [gram_matrix, weighted_sum[None, :], moment[None, :], total_rows], axis=0
        )

    per_owner = LEAVES // lax.axis_size(LEAF)
    owner_part = sum_in_two_steps(
        lax.map(leaf_terms, jnp.arange(per_owner * lax.axis_size(LEAF))),
        (("leaf_0", "leaf_1"), "leaf_2"),
        0,
    )
    owner_sums = total_of(owner_part, "doc")
    own_coefs, own_intercepts = jax.vmap(solve_leaf)(owner_sums)
    coefficients, intercepts = in_one_piece((own_coefs, own_intercepts), LEAF, 0, 1)
    per_leaf = (
        jnp.dot(features.astype(jnp.float32), coefficients.T, precision=lax.Precision.HIGHEST)
        + intercepts[None, :]
    )
    chosen = leaf_ids[:, None] == jnp.arange(LEAVES)[None, :]
    tree_output = jnp.sum(jnp.where(chosen, per_leaf, 0.0), axis=1)
    new_scores = scores + SHRINKAGE * tree_output
    return (gradients, tree_output, new_scores)


def solution(mesh):
    torus = Mesh(
        mesh.devices.reshape(mesh.shape["doc"], 4, 2, 2), ("doc", "leaf_0", "leaf_1", "leaf_2")
    )
    return jax.shard_map(
        body,
        mesh=torus,
        in_specs=(
            P(DOC_LEAF, None),
            P(DOC_LEAF),
            P(DOC_LEAF),
            P(DOC_LEAF),
            P(DOC_LEAF),
            P(DOC_LEAF),
        ),
        out_specs=(P(DOC_LEAF), P(DOC_LEAF), P(DOC_LEAF)),
        check_vma=False,
    )
```

profile of v0, /device:TPU:1, one launch (start us, length us, event | category | flops | bytes accessed | tf_op | source)
XLA Modules:
  0.0 319.7 jit_solution(7557472957276316765)
XLA Ops:
  3.4 6.2 %collective-permute-start = (f32[4,128]{1,0:T(4,128)S(1)}, f32[4,128]{1,0:T(4,128)S(1)}, u32[]{:S(2)}, u32[]{:S(2)}) collective-permute-start(f32[4,128]{1,0:T(4,128)S(1)} %get-tuple-element.294), channel_id=1, source_target_pairs={{0,1},{1,2},{2,3},{3,4},{4,5},{5,6},{6,7},{7,8},{8,9},{9,10},{10,1... | collective-permute-start | bytes 6152 | tf_op jit(solution)/shard_map/ppermute | solution.py:22
  11.6 4.4 %collective-permute-done.1 = f32[4,128]{1,0:T(4,128)S(1)} collective-permute-done((f32[4,128]{1,0:T(4,128)S(1)}, f32[4,128]{1,0:T(4,128)S(1)}, u32[]{:S(2)}, u32[]{:S(2)}) %collective-permute-start.1) | collective-permute-done | bytes 2080 | tf_op jit(solution)/shard_map/ppermute | solution.py:22
  16.7 17.2 %while.32 = (s32[]{:T(128)}, f32[2,512]{1,0:T(2,128)S(1)}, f32[2,512]{1,0:T(2,128)S(1)}, s32[2]{0:T(128)S(1)}, f32[4,1280]{1,0:T(4,128)S(1)}, /*index=5*/s32[]{:...) while((s32[]{:T(128)}, f32[2,512]{1,0:T(2,128)S(1)}, ...), condition=%wide.region_9.10_spmd.clone, body=%wide.region_0.9_spmd.sunk.clone.sunk | while | flops 14173452 | bytes 159045 | solution.py:162
  20.8 3.0 multiply_reduce_fusion.5
  29.4 3.0 multiply_reduce_fusion.5
  34.0 109.2 %while.30 = (s32[]{:T(128)}, f32[16,264,256]{2,1,0:T(8,128)}, s32[16]{0:T(128)S(1)}, s32[1024]{0:T(1024)S(1)}, f32[1024]{0:T(1024)S(1)}, /*index=5*/bf16[1024,25...) while((s32[]{:T(128)}, f32[16,264,256]{2,1,0:T(8,128)}, s32[16]{0:T(128)S(1)}, ...), condition=%wide.region_14.15_spmd, body=%wide.region_10.14_spmd.sunk | while | flops 137047808 | bytes 2423457 | solution.py:188
  37.2 2.0 scatter.13
  44.0 2.0 scatter.13
  57.6 2.0 scatter.13
  64.4 2.0 scatter.13
  78.1 2.0 scatter.13
  91.8 2.0 scatter.13
  98.6 2.0 scatter.13
  105.4 2.0 scatter.13
  112.3 2.0 scatter.13
  119.1 2.0 scatter.13
  125.9 2.0 scatter.13
  132.7 2.0 scatter.13
  139.6 2.0 scatter.13
  143.3 2.6 copy.24
  145.9 7.9 %all_to_all.25 = f32[2,8,1,264,256]{4,3,1,2,0:T(8,128)} all-to-all(f32[2,8,1,264,256]{4,3,1,2,0:T(8,128)S(1)} %copy.24), channel_id=1, replica_groups=mesh['doc'=16,'leaf_0'=4,'leaf_1'=2,'leaf_2'=2] {'leaf_2'}, dimensions={0} | all-to-all | bytes 8650752 | tf_op jit(solution)/shard_map/all_to_all | solution.py:33
  153.8 2.8 reduce_sum.181
  156.6 33.5 %all_to_all.26 = f32[8,1,264,256]{3,2,1,0:T(8,128)} all-to-all(f32[8,1,264,256]{3,2,1,0:T(8,128)S(1)} %bitcast.201), channel_id=1, replica_groups=mesh['doc'=16,'leaf_0'=4,'leaf_1'=2,'leaf_2'=2] {'leaf_0','leaf_1'}, dimensions={0} | all-to-all | bytes 4325376 | tf_op jit(solution)/shard_map/all_to_all | solution.py:40
  192.1 19.8 %all_to_all.27 = f32[16,1,4224]{2,1,0:T(1,128)S(1)} all-to-all(f32[16,1,4224]{2,1,0:T(1,128)S(1)} %all_to_all.18), channel_id=1, replica_groups=mesh['doc'=16,'leaf_0'=4,'leaf_1'=2,'leaf_2'=2] {'doc'}, dimensions={0} | all-to-all | bytes 540672 | tf_op jit(solution)/shard_map/all_to_all | solution.py:33
  213.0 3.7 %all-to-all-start.3 = ((f32[16,1,4224]{2,1,0:T(1,128)}), f32[16,1,4224]{2,1,0:T(1,128)S(1)}, u32[]{:S(2)}, u32[]{:S(2)}) async-start(f32[16,1,4224]{2,1,0:T(1,128)} %broadcast_in_dim.94), calls=%async_computation.3 | async-start | bytes 540672 | tf_op jit(solution)/shard_map/all_to_all | solution.py:56
  216.7 9.9 %all-to-all-done.3 = f32[16,1,4224]{2,1,0:T(1,128)S(1)} async-done(((f32[16,1,4224]{2,1,0:T(1,128)}), f32[16,1,4224]{2,1,0:T(1,128)S(1)}, u32[]{:S(2)}, u32[]{:S(2)}) %all-to-all-start.3) | async-done | bytes 270368 | tf_op jit(solution)/shard_map/all_to_all | solution.py:56
  229.9 11.7 %custom-call.18 = f32[1,128,128]{2,1,0:T(8,128)S(1)} custom-call(f32[1,128,128]{2,1,0:T(8,128)S(1)} %cholesky.117), custom_call_target="Cholesky" | custom-call | tf_op jit(solution)/shard_map/vmap(jit(cholesky))/cholesky | solution.py:130
  241.7 9.8 %custom-call.19 = f32[1,1,128,128]{2,3,1,0:T(8,128)S(1)} custom-call(f32[1,1,128,128]{3,2,1,0:T(8,128)S(1)} %get-tuple-element.293), custom_call_target="InvertDiagBlocksLowerTriangular" | custom-call | tf_op jit(solution)/shard_map/vmap(jit(cholesky))/cholesky | solution.py:130
  252.0 11.7 %custom-call.20 = f32[1,128,128]{2,1,0:T(8,128)S(1)} custom-call(f32[1,128,128]{2,1,0:T(8,128)S(1)} %fusion.8), custom_call_target="Cholesky" | custom-call | tf_op jit(solution)/shard_map/vmap(jit(cholesky))/cholesky | solution.py:130
  265.7 3.8 %while.31 = (s32[]{:T(128)}, f32[1,256,256]{2,1,0:T(8,128)S(1)}, s32[2,2]{1,0:T(2,128)S(1)}, f32[2,1,128,128]{3,2,1,0:T(8,128)S(1)}, s32[]{:T(128)}) while((s32[]{:T(128)}, f32[1,256,256]{2,1,0:T(8,128)S(1)}, s32[2,2]{1,0:T(2,128)S(1)}, f32[2,1,128,128]{3,2,1,0:T(8,128)S(1)}, s32[]{:T(128)}) %tuple.126), condition=%wide.while_cond.2, body=%wide.while_body.2.sunk | while | flops 2 | bytes 131181 | solution.py:132
  269.5 19.9 %custom-call.21 = f32[1,2,128,128]{2,3,1,0:T(8,128)S(1)} custom-call(f32[1,2,128,128]{3,2,1,0:T(8,128)S(1)} %bitcast.233), custom_call_target="InvertDiagBlocksLowerTriangular" | custom-call | tf_op jit(solution)/shard_map/vmap()/triangular_solve | solution.py:132
  292.6 25.8 %all-gather = f32[16,1,257]{2,1,0:T(1,128)S(1)} all-gather(f32[1,1,257]{2,1,0:T(1,128)S(1)} %maximum_bitcast_fusion.1), channel_id=1, replica_groups=mesh['doc'=16,'leaf_0'=4,'leaf_1'=2,'leaf_2'=2] {'leaf_0','leaf_1','leaf..., dimensions={0}, use_global_device_ids=true | all-gather | bytes 17476 | tf_op jit(solution)/shard_map/all_gather | solution.py:77
  (272 shorter events, 106.5 us)
Async XLA Ops:
  3.4 8.2 %collective-permute-start = (f32[4,128]{1,0:T(4,128)S(1)}, f32[4,128]{1,0:T(4,128)S(1)}, u32[]{:S(2)}, u32[]{:S(2)}) collective-permute-start(f32[4,128]{1,0:T(4,128)S(1)} %get-tuple-element.294), channel_id=1, source_target_pairs={{0,1},{1,2},{2,3},{3,4},{4,5},{5,6},{6,7},{7,8},{8,9},{9,10},{10,1... | collective-permute-start | bytes 6152 | tf_op jit(solution)/shard_map/ppermute | solution.py:22
  9.6 6.4 %collective-permute-start.1 = (f32[4,128]{1,0:T(4,128)S(1)}, f32[4,128]{1,0:T(4,128)S(1)}, u32[]{:S(2)}, u32[]{:S(2)}) collective-permute-start(f32[4,128]{1,0:T(4,128)S(1)} %get-tuple-element.295), channel_id=1, source_target_pairs={{1,0},{2,1},{3,2},{4,3},{5,4},{6,5},{7,6},{8,7},{9,8},{10,9},{11,1... | collective-permute-start | bytes 6152 | tf_op jit(solution)/shard_map/ppermute | solution.py:22
  16.7 17.3 %copy-start = (bf16[1024,256]{1,0:T(8,128)(2,1)S(1)}, bf16[1024,256]{1,0:T(8,128)(2,1)}, u32[]{:S(2)}) copy-start(bf16[1024,256]{1,0:T(8,128)(2,1)} %param.15) | copy-start | bytes 1572868
  16.7 17.3 %copy-start.2 = (s32[1024]{0:T(1024)S(1)}, s32[1024]{0:T(1024)}, u32[]{:S(2)}) copy-start(s32[1024]{0:T(1024)} %param.20) | copy-start | bytes 12292
  143.3 2.6 copy-start.1
  213.0 13.6 %all-to-all-start.3 = ((f32[16,1,4224]{2,1,0:T(1,128)}), f32[16,1,4224]{2,1,0:T(1,128)S(1)}, u32[]{:S(2)}, u32[]{:S(2)}) async-start(f32[16,1,4224]{2,1,0:T(1,128)} %broadcast_in_dim.94), calls=%async_computation.3 | async-start | bytes 540672 | tf_op jit(solution)/shard_map/all_to_all | solution.py:56
  241.7 77.4 %copy-start.3 = (f32[1024]{0:T(1024)S(1)}, f32[1024]{0:T(1024)}, u32[]{:S(2)}) copy-start(f32[1024]{0:T(1024)} %param.16) | copy-start | bytes 12292
  319.1 0.6 copy-start.4
where the time goes:
time: 321 us; the launch traced here: 320 us
  other arithmetic  110 us (34%)
  blocking collectives  87 us (27%)
  local copies, waits for them, and re-layouts  71.4 us (22%)
  waiting for transfers between devices  14.3 us (4%)
  matrix products  13.6 us (4%)
  starting transfers between devices  11.8 us (4%)
  loops' own time  6.97 us (2%)
  between operations  4.2 us (1%)
    scatter x32, local copies, waits for them, and re-layouts, leaf_terms(): total_rows = total_rows.at[0, 0].set(jnp.sum(hessians * in_leaf)).at[0, 1...  42.5 us
    another operation x6, other arithmetic, solve_leaf(): factor = jnp.linalg.cholesky(system)  34 us
    all_to_all x1, blocking collectives, sum_in_two_steps(): return jnp.sum(lax.all_to_all(own, far, 0, 0, tiled=True), axis=0)  33.5 us
    all_to_all x2, blocking collectives, sent_and_summed(): lax.all_to_all(pieces, axis, split_axis=0, concat_axis=0, tiled=True)  27.7 us
    all_gather x1, blocking collectives, in_one_piece(): out = lax.all_gather(both, axis, axis=dim, tiled=True)  25.8 us
    another operation x3, other arithmetic, solve_leaf(): lax.linalg.triangular_solve(factor, middle, left_side=True, lower=True, t...  19.9 us
    another operation x38, local copies, waits for them, and re-layouts  13.1 us
    dynamic_update_slice x16, other arithmetic, body(): lax.map(leaf_terms, jnp.arange(per_owner * lax.axis_size(LEAF)))  11.7 us
  transfers between devices with their start and end apart: 3, of which 2 were waited for; matrix products, arithmetic and copies ran while one was open for 0% of the time, Pallas kernels for 0%

commit v1 on v0

v1 whole, which is shorter than its diff:
```python
import jax
import jax.numpy as jnp
from jax import lax
from jax.experimental import pallas as pl
from jax.experimental.pallas import tpu as pltpu
from jax.sharding import Mesh
from jax.sharding import PartitionSpec as P

LEAVES = 16
MAXQ = 128
ROWS = 1024
BLOCKS = ROWS // MAXQ
F = 256
HALF = 128
LEAF_ROWS = 272
DOC_LEAF = ("doc", "leaf_0", "leaf_1", "leaf_2")
LEAF = ("leaf_0", "leaf_1", "leaf_2")
LAMBDA = 1.0
SHRINKAGE = 0.1
F32 = jnp.float32
BF16 = jnp.bfloat16
NT = (((1,), (1,)), ((), ()))
VMEM = pl.BlockSpec(memory_space=pltpu.VMEM)


def iota(shape, dim):
    return lax.broadcasted_iota(jnp.int32, shape, dim)


def discount(rank_values):
    return 1.0 / jnp.log2(1.0 + jnp.maximum(rank_values, 1.0))


def stacked(rows):
    width = rows[0].shape[1]
    sub = iota((8, width), 0)
    out = jnp.zeros((8, width), F32)
    for k, row in enumerate(rows):
        out = jnp.where(sub == k, jnp.broadcast_to(row, (8, width)), out)
    return out


def pair_sums(own, far_cols, far_ge):
    query, gain, disc, score = own
    far_query, far_gain, far_disc, far_score = far_cols
    same = far_query == query
    gain_gap = gain - far_gain
    score_gap = score - far_score
    signed = jnp.where(same, gain_gap * jnp.abs(disc - far_disc), 0.0)
    prob = 1.0 / (1.0 + jnp.exp(jnp.where(gain_gap >= 0.0, score_gap, -score_gap)))
    pull = signed * prob
    grad = jnp.sum(pull, axis=0, keepdims=True)
    hess = jnp.sum(jnp.abs(pull) * (1.0 - prob), axis=0, keepdims=True)
    mates = jnp.where(same, 1.0, 0.0).astype(BF16)
    counts = jnp.dot(far_ge, mates, preferred_element_type=F32)
    return grad, hess, counts


def far_block(query, label, rank, score):
    gain = jnp.exp2(label)
    disc = discount(rank)
    turned = stacked([query, gain, disc, score]).T
    cols = [jnp.broadcast_to(turned[:, c : c + 1], (MAXQ, MAXQ)) for c in range(4)]
    level = (iota((16, MAXQ), 0) + 1).astype(F32)
    at_least = jnp.where(jnp.broadcast_to(label, (16, MAXQ)) >= level, 1.0, 0.0).astype(BF16)
    return cols, at_least


def lambdas(query_ref, label_ref, rank_ref, score_ref, halo):
    query = query_ref[...].astype(F32)
    label = label_ref[...].astype(F32)
    rank = rank_ref[...].astype(F32)
    score = score_ref[...]
    gain = jnp.exp2(label)
    disc = discount(rank)
    own = [[x[k : k + 1, :] for x in (query, gain, disc, score)] for k in range(BLOCKS)]
    sums = [None] * BLOCKS

    def meet(k, far):
        new = pair_sums(own[k], *far)
        sums[k] = new if sums[k] is None else tuple(a + b for a, b in zip(sums[k], new))

    for j in range(BLOCKS):
        far = far_block(*[x[j : j + 1, :] for x in (query, label, rank, score)])
        for k in (j - 1, j, j + 1):
            if 0 <= k < BLOCKS:
                meet(k, far)
    before, after = halo()
    meet(0, far_block(*[before[c : c + 1, :] for c in range(4)]))
    meet(BLOCKS - 1, far_block(*[after[c : c + 1, :] for c in range(4)]))

    position = (iota((MAXQ, MAXQ), 0) + 1).astype(F32)
    disc_at = discount(position)
    grads, hess = [], []
    for k in range(BLOCKS):
        pull, push, counts = sums[k]
        ideal = jnp.zeros((1, MAXQ), F32)
        for level in range(4):
            inside = jnp.where(position <= counts[level : level + 1, :], disc_at, 0.0)
            ideal = ideal + float(2**level) * jnp.sum(inside, axis=0, keepdims=True)
        inverse = 1.0 / jnp.maximum(ideal, 1.0)
        grads.append(-inverse * pull)
        hess.append(inverse * push)
    return grads, hess


def leaf_inputs(features_ref, leaf_ref, grads, hess, weighted_ref, in_leaf_ref, sums_ref):
    leaf = leaf_ref[...]
    grad_low = []
    h_lanes = jnp.zeros((LEAVES, MAXQ), F32)
    g_lanes = jnp.zeros((LEAVES, MAXQ), F32)
    for k in range(BLOCKS):
        rows = slice(MAXQ * k, MAXQ * (k + 1))
        turned = features_ref[rows, :].astype(F32).T
        weighted_ref[:, rows] = (turned * hess[k]).astype(BF16)
        in_leaf = jnp.where(
            jnp.broadcast_to(leaf[k : k + 1, :], (LEAVES, MAXQ)) == iota((LEAVES, MAXQ), 0),
            1.0,
            0.0,
        )
        in_leaf_ref[:, rows] = in_leaf
        h_lanes = h_lanes + in_leaf * hess[k]
        g_lanes = g_lanes + in_leaf * grads[k]
        grad_low.append((in_leaf * grads[k]).astype(BF16))
    moment = jnp.dot(
        jnp.concatenate(grad_low, axis=1), features_ref[...], preferred_element_type=F32
    )
    hsum = lax.dot_general(
        in_leaf_ref[...].astype(BF16), weighted_ref[...], NT, preferred_element_type=F32
    )
    wide = (LEAVES, MAXQ)
    sums_ref[0] = hsum[:, :HALF]
    sums_ref[1] = hsum[:, HALF:]
    sums_ref[2] = moment[:, :HALF]
    sums_ref[3] = moment[:, HALF:]
    sums_ref[4] = jnp.broadcast_to(jnp.sum(h_lanes, axis=1, keepdims=True), wide)
    sums_ref[5] = jnp.broadcast_to(jnp.sum(g_lanes, axis=1, keepdims=True), wide)


def leaf_gram(number, features_ref, weighted_ref, in_leaf_ref):
    mask = jnp.broadcast_to(in_leaf_ref[pl.ds(number, 1), :], (16, ROWS)).astype(BF16)
    own = (weighted_ref[...].reshape(16, 16, ROWS) * mask[None]).reshape(F, ROWS)
    return jnp.dot(own, features_ref[...], preferred_element_type=F32)


def packed_leaf(gram, number, sums_ref):
    row = iota((HALF, HALF), 0)
    col = iota((HALF, HALF), 1)
    last = gram[HALF:, HALF:]
    mixed = jnp.where(col <= row, gram[:HALF, :HALF], last)
    diag = jnp.sum(jnp.where(col == row, last, 0.0), axis=0, keepdims=True)
    small = [sums_ref[k, pl.ds(number, 1), :] for k in range(6)]
    extra = stacked(small + [diag])
    first = jnp.concatenate(
        [mixed[:64], extra, mixed[64:], jnp.zeros((8, HALF), F32)], axis=0
    )
    return first, gram[HALF:, :HALF]


def dotted(a, b, dims=(((1,), (0,)), ((), ()))):
    return lax.dot_general(
        a, b, dims, precision=lax.Precision.HIGHEST, preferred_element_type=F32
    )


def small_inverse(d):
    p = len(d)
    if p == 1:
        return [[1.0 / d[0][0]]]
    if p == 2:
        a, b, c = d[0][0], d[0][1], d[1][1]
        r = 1.0 / (a * c - b * b)
        n = -b * r
        return [[c * r, n], [n, a * r]]
    h = p // 2

    def dot(xs, ys):
        total = xs[0] * ys[0]
        for x, y in zip(xs[1:], ys[1:]):
            total = total + x * y
        return total

    first = small_inverse([line[:h] for line in d[:h]])
    side = [line[h:] for line in d[:h]]
    u = [[dot(first[i], [side[m][j] for m in range(h)]) for j in range(h)] for i in range(h)]
    rest = [[None] * h for _ in range(h)]
    for i in range(h):
        for j in range(i, h):
            rest[i][j] = rest[j][i] = d[h + i][h + j] - dot(
                [side[m][i] for m in range(h)], [u[m][j] for m in range(h)]
            )
    last = small_inverse(rest)
    out = [[None] * p for _ in range(p)]
    for i in range(h):
        for j in range(h):
            out[h + i][h + j] = last[i][j]
            out[i][h + j] = out[h + j][i] = -dot(u[i], [last[m][j] for m in range(h)])
    for i in range(h):
        for j in range(i, h):
            out[i][j] = out[j][i] = first[i][j] - dot(
                [out[i][h + m] for m in range(h)], [u[j][m] for m in range(h)]
            )
    return out


def spd_inverse(m, p):
    n = m.shape[0]
    lane = iota((8, n), 1)
    sub = iota((8, n), 0)
    for k in range(0, n, p):
        top = k // 8 * 8
        cols = [jnp.broadcast_to(m[:, k + b : k + b + 1], m.shape) for b in range(p)]
        rows = [jnp.broadcast_to(m[k + a : k + a + 1, :], (8, n)) for a in range(p)]
        d = [[None] * p for _ in range(p)]
        for a in range(p):
            for b in range(a, p):
                d[a][b] = d[b][a] = jnp.broadcast_to(cols[b][k + a : k + a + 1, :], (8, n))
        v = small_inverse(d)
        scaled = []
        for a in range(p):
            r = v[a][0] * rows[0]
            for b in range(1, p):
                r = r + v[a][b] * rows[b]
            for b in range(p):
                r = jnp.where(lane == k + b, v[a][b], r)
            scaled.append(r)
        pivot = (lane >= k) & (lane < k + p)
        tiles = []
        for t in range(0, n, 8):
            tile = jnp.where(pivot, 0.0, m[t : t + 8, :])
            for a in range(p):
                tile = tile - cols[a][t : t + 8, :] * scaled[a]
            if t == top:
                for a in range(p):
                    tile = jnp.where(sub == k - top + a, scaled[a], tile)
            tiles.append(tile)
        m = jnp.concatenate(tiles, axis=0)
    return m


def solved(mixed, extra, low):
    row = iota((HALF, HALF), 0)
    col = iota((HALF, HALF), 1)
    turned = mixed.T
    hsum = [extra[0:1, :], extra[1:2, :]]
    moment = [extra[2:3, :], extra[3:4, :]]
    htotal, gtotal, diag = extra[4:5, :], extra[5:6, :], extra[6:7, :]
    share = 1.0 / (htotal + LAMBDA)
    scaled = [h * share for h in hsum]
    across = stacked(hsum).T
    over = [jnp.broadcast_to(across[:, k : k + 1], (HALF, HALF)) for k in range(2)]
    unit = jnp.where(row == col, LAMBDA, 0.0)
    a11 = jnp.where(col <= row, mixed, turned) + unit - over[0] * scaled[0]
    a21 = low - over[1] * scaled[0]
    a22 = jnp.where(col > row, mixed, jnp.where(col < row, turned, diag))
    a22 = a22 + unit - over[1] * scaled[1]
    side = [scaled[k] * gtotal - moment[k] for k in range(2)]
    inv1 = spd_inverse(a11, 8)
    z = dotted(a21, inv1)
    inv2 = spd_inverse(a22 - dotted(z, a21, NT), 8)
    b1 = jnp.broadcast_to(side[0], (8, HALF))
    b2 = jnp.broadcast_to(side[1], (8, HALF))
    w2 = dotted(b2 - dotted(b1, z, NT), inv2)
    w1 = dotted(b1, inv1) - dotted(w2, z)
    total = jnp.sum(hsum[0] * w1 + hsum[1] * w2, axis=1, keepdims=True)
    c = -(gtotal + total) * share
    return stacked([w1[0:1], w2[0:1], c[0:1]])


def leaf_output(features_ref, leaf_ref, score_ref, weights, intercepts, tree_ref, new_ref):
    high = weights.astype(BF16)
    left = weights - high.astype(F32)
    mid = left.astype(BF16)
    low = (left - mid.astype(F32)).astype(BF16)
    parts = jnp.concatenate([high, mid, low], axis=0)
    sums = lax.dot_general(parts, features_ref[...], NT, preferred_element_type=F32)
    per_leaf = sums[:16] + sums[16:32] + sums[32:48]
    leaf = leaf_ref[...]
    for k in range(BLOCKS):
        rows = slice(MAXQ * k, MAXQ * (k + 1))
        own = jnp.broadcast_to(leaf[k : k + 1, :], (LEAVES, MAXQ)) == iota((LEAVES, MAXQ), 0)
        tree = jnp.sum(
            jnp.where(own, per_leaf[:, rows] + intercepts, 0.0), axis=0, keepdims=True
        )
        tree_ref[k : k + 1, :] = tree
        new_ref[k : k + 1, :] = score_ref[k : k + 1, :] + SHRINKAGE * tree


def terms_kernel(
    features, score, label, query, rank, leaf, before, after, grad_out, packed, weighted, in_leaf, sums
):
    grads, hess = lambdas(query, label, rank, score, lambda: (before[...], after[...]))
    for k in range(BLOCKS):
        grad_out[k : k + 1, :] = grads[k]
    leaf_inputs(features, leaf, grads, hess, weighted, in_leaf, sums)

    def one(number, carry):
        first, second = packed_leaf(leaf_gram(number, features, weighted, in_leaf), number, sums)
        packed[number, :144, :] = first
        packed[number, 144:, :] = second
        return carry

    lax.fori_loop(0, LEAVES, one, 0)


def solve_kernel(packed, out):
    block = packed[...]
    mixed = jnp.concatenate([block[:64], block[72:136]], axis=0)
    out[...] = solved(mixed, block[64:72], block[144:])


def output_kernel(features, leaf, score, coefs, tree, new):
    all_rows = coefs[...]
    weights = jnp.concatenate([all_rows[0], all_rows[1]], axis=1)
    leaf_output(features, leaf, score, weights, all_rows[2], tree, new)


def passed_along(value, axis, by):
    devices = lax.axis_size(axis)
    return lax.ppermute(value, axis, [(i, (i + by) % devices) for i in range(devices)])


def body(features, scores, labels, query_ids, ranks, leaf_ids):
    lines = [x.reshape(BLOCKS, MAXQ) for x in (scores, labels, query_ids, ranks, leaf_ids)]
    score, label, query, rank, leaf = lines
    info = jnp.stack([x.astype(F32) for x in (query, label, rank, score)])
    index = lax.axis_index(DOC_LEAF)
    before = passed_along(info[:, BLOCKS - 1], DOC_LEAF, 1)
    after = passed_along(info[:, 0], DOC_LEAF, -1)
    none = jnp.full((1, MAXQ), -1.0, F32)
    before = jnp.where((index == 0) & (jnp.arange(4)[:, None] == 0), none, before)
    after = jnp.where(
        (index == lax.axis_size(DOC_LEAF) - 1) & (jnp.arange(4)[:, None] == 0), none, after
    )
    grads, packed = pl.pallas_call(
        terms_kernel,
        out_shape=[
            jax.ShapeDtypeStruct((BLOCKS, MAXQ), F32),
            jax.ShapeDtypeStruct((LEAVES, LEAF_ROWS, HALF), F32),
        ],
        in_specs=[VMEM] * 8,
        out_specs=[VMEM] * 2,
        scratch_shapes=[
            pltpu.VMEM((F, ROWS), BF16),
            pltpu.VMEM((LEAVES, ROWS), F32),
            pltpu.VMEM((6, LEAVES, MAXQ), F32),
        ],
    )(features, score, label, query, rank, leaf, before, after)
    part = lax.psum_scatter(packed, LEAF, scatter_dimension=0, tiled=False)
    total = lax.psum(part, "doc")
    coefs = pl.pallas_call(
        solve_kernel,
        out_shape=jax.ShapeDtypeStruct((8, HALF), F32),
        in_specs=[VMEM],
        out_specs=VMEM,
    )(total)
    gathered = lax.all_gather(coefs, LEAF, axis=1)
    tree, new = pl.pallas_call(
        output_kernel,
        out_shape=[jax.ShapeDtypeStruct((BLOCKS, MAXQ), F32)] * 2,
        in_specs=[VMEM] * 4,
        out_specs=[VMEM] * 2,
    )(features, leaf, score, gathered)
    return grads.reshape(ROWS), tree.reshape(ROWS), new.reshape(ROWS)


def solution(mesh):
    torus = Mesh(
        mesh.devices.reshape(mesh.shape["doc"], 4, 2, 2), ("doc", "leaf_0", "leaf_1", "leaf_2")
    )
    spec = P(DOC_LEAF)
    return jax.shard_map(
        body,
        mesh=torus,
        in_specs=(P(DOC_LEAF, None), spec, spec, spec, spec, spec),
        out_specs=(spec, spec, spec),
        check_vma=False,
    )
```

time: 321 us -> 292 us (0.910)
  waiting for transfers between devices: 14.3 us -> 208 us
  other arithmetic: 110 us -> 4.06 us
  local copies, waits for them, and re-layouts: 71.4 us -> 0.63 us
  blocking collectives: 87 us -> 35.9 us
  Pallas kernels: 0 us -> 24 us
  matrix products: 13.6 us -> 0 us
  between operations: 4.2 us -> 14 us
  starting transfers between devices: 11.8 us -> 4.72 us
  loops' own time: 6.97 us -> 0 us
    psum x0 -> x1, waiting for transfers between devices: none -> 125 us  [body(): total = lax.psum(part, 'doc')]
    reduce_scatter x0 -> x1, waiting for transfers between devices: none -> 76.8 us  [body(): part = lax.psum_scatter(packed, LEAF, scatter_dimension=0, tiled=False)]
    all_to_all x3 -> x0, blocking collectives: 61.2 us -> none  [the longest x1 33.5 us: sum_in_two_steps(): return jnp.sum(lax.all_to_all(own, far, 0, 0, tiled=True), axis=0)]
    another operation x13 -> x0, other arithmetic: 53.9 us -> none  [the longest x6 34 us: solve_leaf(): factor = jnp.linalg.cholesky(system)]
    scatter x32 -> x0, local copies, waits for them, and re-layouts: 42.5 us -> none  [leaf_terms(): total_rows = total_rows.at[0, 0].set(jnp.sum(hessians * in_leaf)).at[0, 1...]
    reduce_sum x42 -> x0, other arithmetic: 27.9 us -> none  [the longest x16 10.2 us: leaf_terms(): jnp.sum(hessians * in_leaf)]
    pallas_call x0 -> x3, Pallas kernels: none -> 24 us  [the longest x1 12.3 us: body(): pl.pallas_call(solve_kernel, out_shape=jax.ShapeDtypeStruct((8, HALF), F3...]
    another operation x42 -> x0, local copies, waits for them, and re-layouts: 13.3 us -> none
  transfers between devices with their start and end apart: 3 -> 4, of which waited for: 2 -> 4; matrix products, arithmetic and copies ran while one was open for 0% -> 0% of each run, Pallas kernels for 0% -> 0%
where the time goes in v1:
time: 292 us
  waiting for transfers between devices  208 us (71%)
  blocking collectives  35.9 us (12%)
  Pallas kernels  24 us (8%)
  between operations  14 us (5%)
  starting transfers between devices  4.72 us (2%)
  other arithmetic  4.06 us (1%)
    psum x1, waiting for transfers between devices, body(): total = lax.psum(part, 'doc')  125 us
    reduce_scatter x1, waiting for transfers between devices, body(): part = lax.psum_scatter(packed, LEAF, scatter_dimension=0, tiled=False)  76.8 us
    all_gather x1, blocking collectives, body(): gathered = lax.all_gather(coefs, LEAF, axis=1)  35.9 us
    pallas_call x1, Pallas kernels, body(): pl.pallas_call(solve_kernel, out_shape=jax.ShapeDtypeStruct((8, HALF), F3...  12.3 us
    pallas_call x1, Pallas kernels, body(): pl.pallas_call(terms_kernel, out_shape=[jax.ShapeDtypeStruct((BLOCKS, MAX...  9.74 us
    ppermute x2, waiting for transfers between devices, passed_along(): lax.ppermute(value, axis, [(i, (i + by) % devices) for i in range(devices)])  7.04 us
  transfers between devices with their start and end apart: 4, of which 4 were waited for; matrix products, arithmetic and copies ran while one was open for 0% of the time, Pallas kernels for 0%

profile of v1, /device:TPU:1, one launch (start us, length us, event | category | flops | bytes accessed | tf_op | source)
XLA Modules:
  0.0 291.8 jit_solution(4095541045920997398)
XLA Ops:
  7.2 0.0 reduce-scatter.2.cloned.1.call-start
  7.2 0.7 convert_element_type.41
  7.9 0.7 convert_element_type.39
  8.6 0.7 convert_element_type.43
  9.3 0.7 fusion
  10.0 3.3 %collective-permute-start.1 = (f32[4,128]{1,0:T(4,128)S(1)}, f32[4,128]{1,0:T(4,128)S(1)}, u32[]{:S(2)}, u32[]{:S(2)}) collective-permute-start(f32[4,128]{1,0:T(4,128)S(1)} %get-tuple-element.11), channel_id=1, source_target_pairs={{0,255},{1,0},{2,1},{3,2},{4,3},{5,4},{6,5},{7,6},{8,7},{9,8},{10,... | collective-permute-start | bytes 6152 | tf_op jit(solution)/shard_map/ppermute | solution.py:320
  13.2 1.2 collective-permute-start
  14.4 1.2 collective-permute-done.1
  15.6 0.6 broadcast_select_fusion.after
  16.3 5.9 %collective-permute-done = f32[4,128]{1,0:T(4,128)S(1)} collective-permute-done((f32[4,128]{1,0:T(4,128)S(1)}, f32[4,128]{1,0:T(4,128)S(1)}, u32[]{:S(2)}, u32[]{:S(2)}) %collective-permute-start) | collective-permute-done | bytes 2080 | tf_op jit(solution)/shard_map/ppermute | solution.py:320
  22.1 0.6 broadcast_select_fusion.1.before
  22.8 9.7 %shard_map.85 = (f32[8,128]{1,0:T(8,128)}, f32[16,272,128]{2,1,0:T(8,128)}) custom-call(bf16[1024,256]{1,0:T(8,128)(2,1)} %features.3, f32[8,128]{1,0:T(8,128)} %bitcast.25, s32[8,128]{1,0:T(8,128)} %bitcast.29, s32[8,128]{1,0:T(8,128)} %bitcast.30, s32[8,128]{1,0:T(8,128)} %bitcast.31, s32[8,128]{1,0:T(8,128)} %bitcast.27, ...), custom_call_target="tpu_custom_call" | custom-call | tf_op jit(solution)/shard_map/pallas_call | solution.py:335
  32.5 0.0 reduce-scatter.2.cloned.1.call-update
  32.5 0.2 all-reduce.2.cloned.1.call-start
  32.8 76.8 %reduce-scatter.2.cloned.1.call-done = f32[1,272,128]{2,1,0:T(8,128)} async-done(((f32[16,272,128]{2,1,0:T(8,128)}), f32[1,272,128]{2,1,0:T(8,128)}) %reduce-scatter.2.cloned.1.call-update) | async-done | bytes 139280 | tf_op jit(solution)/shard_map/reduce_scatter | solution.py:349
  109.6 0.0 all-reduce.2.cloned.1.call-update
  109.6 124.5 %all-reduce.2.cloned.1.call-done.packed = f32[272,128]{1,0:T(8,128)} async-done(((f32[272,128]{1,0:T(8,128)}), f32[272,128]{1,0:T(8,128)}) %all-reduce.2.cloned.1.call-update) | async-done | bytes 139280 | tf_op jit(solution)/shard_map/psum | solution.py:350
  234.2 12.3 %shard_map.86 = f32[8,128]{1,0:T(8,128)} custom-call(f32[272,128]{1,0:T(8,128)} %all-reduce.2.cloned.1.call-done.packed), custom_call_target="tpu_custom_call" | custom-call | tf_op jit(solution)/shard_map/pallas_call | solution.py:351
  246.5 35.9 %all-gather = f32[8,2048]{1,0:T(8,128)S(1)} all-gather(f32[8,128]{1,0:T(8,128)} %shard_map.86), channel_id=2, replica_groups=mesh['doc'=16,'leaf_0'=4,'leaf_1'=2,'leaf_2'=2] {'leaf_0','leaf_1','leaf..., dimensions={1}, use_global_device_ids=true | all-gather | bytes 69632 | tf_op jit(solution)/shard_map/all_gather | solution.py:357
  282.4 0.6 copy.11
  283.0 1.9 shard_map.87
  (2 shorter events, 0.0 us)
Async XLA Ops:
  7.2 102.4 %reduce-scatter.2.cloned.1.call-start = ((), (), s32[]{:S(2)}) async-start(), calls=%async_computation.1 | async-start | bytes 2367488 | tf_op jit(solution)/shard_map/reduce_scatter | solution.py:349
  10.0 5.6 %collective-permute-start.1 = (f32[4,128]{1,0:T(4,128)S(1)}, f32[4,128]{1,0:T(4,128)S(1)}, u32[]{:S(2)}, u32[]{:S(2)}) collective-permute-start(f32[4,128]{1,0:T(4,128)S(1)} %get-tuple-element.11), channel_id=1, source_target_pairs={{0,255},{1,0},{2,1},{3,2},{4,3},{5,4},{6,5},{7,6},{8,7},{9,8},{10,... | collective-permute-start | bytes 6152 | tf_op jit(solution)/shard_map/ppermute | solution.py:320
  13.2 8.9 %collective-permute-start = (f32[4,128]{1,0:T(4,128)S(1)}, f32[4,128]{1,0:T(4,128)S(1)}, u32[]{:S(2)}, u32[]{:S(2)}) collective-permute-start(f32[4,128]{1,0:T(4,128)S(1)} %get-tuple-element.12), channel_id=1, source_target_pairs={{0,1},{1,2},{2,3},{3,4},{4,5},{5,6},{6,7},{7,8},{8,9},{9,10},{10,1... | collective-permute-start | bytes 6152 | tf_op jit(solution)/shard_map/ppermute | solution.py:320
  32.5 201.6 %all-reduce.2.cloned.1.call-start = ((), (), s32[]{:S(2)}) async-start(), calls=%async_computation.2 | async-start | bytes 278528 | tf_op jit(solution)/shard_map/psum | solution.py:350
Sparse Core Ops, SparseCore 0:
  32.7 76.9 reduce-scatter.1
  112.2 121.8 all-reduce.1

commit v2 on v1

--- a/solution.py
+++ b/solution.py
@@ -13,8 +13,9 @@
 F = 256
 HALF = 128
 LEAF_ROWS = 272
-DOC_LEAF = ("doc", "leaf_0", "leaf_1", "leaf_2")
-LEAF = ("leaf_0", "leaf_1", "leaf_2")
+AXES = ("z", "y_lo", "x", "y_hi", "core")
+MESH = pl.DeviceIdType.MESH
+PIVOTS = 4
 LAMBDA = 1.0
 SHRINKAGE = 0.1
 F32 = jnp.float32
@@ -66,34 +67,40 @@
     return cols, at_least
 
 
-def lambdas(query_ref, label_ref, rank_ref, score_ref, halo):
+def own_rows(query_ref, label_ref, rank_ref, score_ref):
     query = query_ref[...].astype(F32)
     label = label_ref[...].astype(F32)
     rank = rank_ref[...].astype(F32)
-    score = score_ref[...]
-    gain = jnp.exp2(label)
-    disc = discount(rank)
-    own = [[x[k : k + 1, :] for x in (query, gain, disc, score)] for k in range(BLOCKS)]
+    return query, label, rank, score_ref[...]
+
+
+def meet(own, sums, k, far):
+    new = pair_sums([x[k : k + 1, :] for x in own], *far)
+    sums[k] = new if sums[k] is None else tuple(a + b for a, b in zip(sums[k], new))
+
+
+def lambdas_within(rows):
+    query, label, rank, score = rows
+    own = (query, jnp.exp2(label), discount(rank), score)
     sums = [None] * BLOCKS
-
-    def meet(k, far):
-        new = pair_sums(own[k], *far)
-        sums[k] = new if sums[k] is None else tuple(a + b for a, b in zip(sums[k], new))
-
     for j in range(BLOCKS):
-        far = far_block(*[x[j : j + 1, :] for x in (query, label, rank, score)])
+        far = far_block(*[x[j : j + 1, :] for x in rows])
         for k in (j - 1, j, j + 1):
             if 0 <= k < BLOCKS:
-                meet(k, far)
-    before, after = halo()
-    meet(0, far_block(*[before[c : c + 1, :] for c in range(4)]))
-    meet(BLOCKS - 1, far_block(*[after[c : c + 1, :] for c in range(4)]))
-
+                meet(own, sums, k, far)
+    return own, sums
+
+
+def lambdas_across(own, sums, before, after):
+    meet(own, sums, 0, far_block(*[before[c : c + 1, :] for c in range(4)]))
+    meet(own, sums, BLOCKS - 1, far_block(*[after[c : c + 1, :] for c in range(4)]))
+
+
+def normalized(sums):
     position = (iota((MAXQ, MAXQ), 0) + 1).astype(F32)
     disc_at = discount(position)
     grads, hess = [], []
-    for k in range(BLOCKS):
-        pull, push, counts = sums[k]
+    for pull, push, counts in sums:
         ideal = jnp.zeros((1, MAXQ), F32)
         for level in range(4):
             inside = jnp.where(position <= counts[level : level + 1, :], disc_at, 0.0)
@@ -225,16 +232,16 @@
                 r = jnp.where(lane == k + b, v[a][b], r)
             scaled.append(r)
         pivot = (lane >= k) & (lane < k + p)
-        tiles = []
-        for t in range(0, n, 8):
-            tile = jnp.where(pivot, 0.0, m[t : t + 8, :])
-            for a in range(p):
-                tile = tile - cols[a][t : t + 8, :] * scaled[a]
-            if t == top:
-                for a in range(p):
-                    tile = jnp.where(sub == k - top + a, scaled[a], tile)
-            tiles.append(tile)
-        m = jnp.concatenate(tiles, axis=0)
+        whole = jnp.where(jnp.broadcast_to(pivot[:1], m.shape), 0.0, m)
+        for a in range(p):
+            whole = whole - cols[a] * jnp.broadcast_to(scaled[a][:1], m.shape)
+        tile = whole[top : top + 8]
+        for a in range(p):
+            tile = jnp.where(sub == k - top + a, scaled[a], tile)
+        parts = [whole[:top]] if top else []
+        parts += [tile]
+        parts += [whole[top + 8 :]] if top + 8 < n else []
+        m = jnp.concatenate(parts, axis=0)
     return m
 
 
@@ -255,9 +262,9 @@
     a22 = jnp.where(col > row, mixed, jnp.where(col < row, turned, diag))
     a22 = a22 + unit - over[1] * scaled[1]
     side = [scaled[k] * gtotal - moment[k] for k in range(2)]
-    inv1 = spd_inverse(a11, 8)
+    inv1 = spd_inverse(a11, PIVOTS)
     z = dotted(a21, inv1)
-    inv2 = spd_inverse(a22 - dotted(z, a21, NT), 8)
+    inv2 = spd_inverse(a22 - dotted(z, a21, NT), PIVOTS)
     b1 = jnp.broadcast_to(side[0], (8, HALF))
     b2 = jnp.broadcast_to(side[1], (8, HALF))
     w2 = dotted(b2 - dotted(b1, z, NT), inv2)
@@ -286,93 +293,348 @@
         new_ref[k : k + 1, :] = score_ref[k : k + 1, :] + SHRINKAGE * tree
 
 
-def terms_kernel(
-    features, score, label, query, rank, leaf, before, after, grad_out, packed, weighted, in_leaf, sums
+def position():
+    z, y_lo, x, y_hi, core = [lax.axis_index(a) for a in AXES]
+    return z, 2 * y_hi + y_lo, x, core
+
+
+def device(z, y, x, core):
+    return (z, lax.rem(y, 2), x, lax.div(y, 2), core)
+
+
+def neighbour(by):
+    index = jnp.int32(0)
+    total = 1
+    for a in AXES:
+        index = index * lax.axis_size(a) + lax.axis_index(a)
+        total *= lax.axis_size(a)
+    index = lax.rem(index + by + total, total)
+    place = []
+    for a in reversed(AXES):
+        place.append(lax.rem(index, lax.axis_size(a)))
+        index = lax.div(index, lax.axis_size(a))
+    return tuple(reversed(place))
+
+
+def ahead(value, by, size):
+    return lax.rem(value + by, size)
+
+
+def level_kernel(
+    features, score, label, query, rank, leaf,
+    out,
+    weighted, in_leaf, sums_ref,
+    edge, before, after,
+    pair_out, pair_in,
+    first_sum, second_sum, first_in, second_in,
+    first_part, second_part, first_in2, second_in2,
+    slab, slab_in, final, first_all, second_all, coef, coefs,
+    halo_send, halo_recv, pair_send, pair_recv,
+    p1x_send, p1x_recv, p1y_send, p1y_recv,
+    p2x_send, p2x_recv, p2y_send, p2y_recv,
+    z_send, z_recv, gx_send, gx_recv, gy_send, gy_recv,
+    w_send, w_recv,
 ):
-    grads, hess = lambdas(query, label, rank, score, lambda: (before[...], after[...]))
+    z, y, x, core = position()
+    depth = lax.axis_size("z")
+    y_lo, x_lo = lax.rem(y, 2), lax.rem(x, 2)
+    y_hi, x_hi = lax.div(y, 2), lax.div(x, 2)
+    y_pair, x_pair = y + 1 - 2 * y_lo, x + 1 - 2 * x_lo
+    other = 1 - core
+    solver = x_lo == y_lo
+    in_plane = [
+        (dx, dy, dc) for dx in (2, 1, 3, 0) for dy in (2, 1, 3, 0) for dc in (1, 0) if dx or dy or dc
+    ]
+
+    def plane(dx, dy, dc):
+        return device(z, ahead(y, dy, 4), ahead(x, dx, 4), ahead(core, dc, 2))
+
+    barrier = pltpu.get_barrier_semaphore()
+    partners = [neighbour(1), neighbour(-1)] + [plane(*d) for d in in_plane]
+    for d in range(1, depth):
+        at = ahead(z, d, depth)
+        partners += [device(at, y, x, core), device(at, y_pair, x, core), device(at, y, x_pair, core)]
+    for partner in partners:
+        pl.semaphore_signal(barrier, inc=1, device_id=partner, device_id_type=MESH)
+
+    def remote(src, dst, send, recv, to):
+        return pltpu.make_async_remote_copy(
+            src_ref=src, dst_ref=dst, send_sem=send, recv_sem=recv, device_id=to, device_id_type=MESH
+        )
+
+    rows = own_rows(query, label, rank, score)
+    edge[0] = stacked([r[BLOCKS - 1 : BLOCKS, :] for r in rows])
+    edge[1] = stacked([r[0:1, :] for r in rows])
+    own, sums = lambdas_within(rows)
+    pl.semaphore_wait(barrier, len(partners))
+
+    later, earlier = neighbour(1), neighbour(-1)
+    to_later = remote(edge.at[0], before, halo_send.at[0], halo_recv.at[0], later)
+    to_earlier = remote(edge.at[1], after, halo_send.at[1], halo_recv.at[1], earlier)
+    to_later.start()
+    to_earlier.start()
+    to_later.wait()
+    to_earlier.wait()
+    first_device = (z == 0) & (y_lo == 0) & (x == 0) & (y_hi == 0) & (core == 0)
+    last_device = (z == depth - 1) & (y_lo == 1) & (x == 3) & (y_hi == 1) & (core == 1)
+    top = iota((8, MAXQ), 0) == 0
+    was = jnp.where(top & first_device, -1.0, before[...])
+    will = jnp.where(top & last_device, -1.0, after[...])
+    lambdas_across(own, sums, was, will)
+    grads, hess = normalized(sums)
     for k in range(BLOCKS):
-        grad_out[k : k + 1, :] = grads[k]
-    leaf_inputs(features, leaf, grads, hess, weighted, in_leaf, sums)
-
-    def one(number, carry):
-        first, second = packed_leaf(leaf_gram(number, features, weighted, in_leaf), number, sums)
-        packed[number, :144, :] = first
-        packed[number, 144:, :] = second
+        out[0, k : k + 1, :] = grads[k]
+    leaf_inputs(features, leaf, grads, hess, weighted, in_leaf, sums_ref)
+
+    def turn(t):
+        return lax.rem(2 * (x + 1) + t, 8)
+
+    def pair_copy(j):
+        return remote(
+            pair_out.at[j], pair_in.at[j], pair_send.at[j], pair_recv.at[j], plane(0, 0, 1)
+        )
+
+    def for_other(t, carry):
+        j = turn(t)
+        number = 8 * other + j
+        first, second = packed_leaf(leaf_gram(number, features, weighted, in_leaf), number, sums_ref)
+        pair_out[j, :144, :] = first
+        pair_out[j, 144:, :] = second
+        pair_copy(j).start()
         return carry
 
-    lax.fori_loop(0, LEAVES, one, 0)
-
-
-def solve_kernel(packed, out):
-    block = packed[...]
-    mixed = jnp.concatenate([block[:64], block[72:136]], axis=0)
-    out[...] = solved(mixed, block[64:72], block[144:])
-
-
-def output_kernel(features, leaf, score, coefs, tree, new):
-    all_rows = coefs[...]
-    weights = jnp.concatenate([all_rows[0], all_rows[1]], axis=1)
-    leaf_output(features, leaf, score, weights, all_rows[2], tree, new)
-
-
-def passed_along(value, axis, by):
-    devices = lax.axis_size(axis)
-    return lax.ppermute(value, axis, [(i, (i + by) % devices) for i in range(devices)])
+    lax.fori_loop(0, 8, for_other, 0)
+
+    def p1x_copy(t):
+        j, d = turn(t), lax.div(t, 2) + 1
+        return remote(
+            first_sum.at[j],
+            first_in.at[d - 1, lax.rem(t, 2)],
+            p1x_send.at[j],
+            p1x_recv.at[d - 1, lax.rem(t, 2)],
+            device(z, y, ahead(x, d, 4), core),
+        )
+
+    def row_of(j):
+        return 2 * lax.rem(j, 2) + lax.rem(lax.div(j, 2), 2)
+
+    def p1y_copy(j):
+        d = lax.rem(row_of(j) - y + 4, 4)
+        return remote(
+            second_sum.at[j],
+            second_in.at[lax.rem(d + 3, 4), lax.div(j, 4)],
+            p1y_send.at[j],
+            p1y_recv.at[lax.rem(d + 3, 4), lax.div(j, 4)],
+            device(z, row_of(j), x, core),
+        )
+
+    def for_own(t, carry):
+        j = turn(t)
+        number = 8 * core + j
+        first, second = packed_leaf(leaf_gram(number, features, weighted, in_leaf), number, sums_ref)
+        pair_copy(j).wait_recv()
+        first_sum[j] = first + pair_in[j, :144, :]
+        second_sum[j] = second + pair_in[j, 144:, :]
+
+        @pl.when(t < 6)
+        def _():
+            p1x_copy(t).start()
+
+        @pl.when(row_of(j) != y)
+        def _():
+            p1y_copy(j).start()
+
+        return carry
+
+    lax.fori_loop(0, 8, for_own, 0)
+
+    for h in range(2):
+        for d in range(1, 4):
+            p1x_copy(2 * (d - 1) + h).wait_recv()
+        total = first_sum[2 * x + h] + first_in[0, h] + first_in[1, h] + first_in[2, h]
+        first_part[2 * h] = total[:72]
+        first_part[2 * h + 1] = total[72:]
+
+    def p2x_copy(d):
+        at = ahead(y, d, 4)
+        return remote(
+            first_part.at[at], first_in2.at[d - 1], p2x_send.at[d - 1], p2x_recv.at[d - 1],
+            device(z, at, x, core),
+        )
+
+    def p2y_copy(d):
+        at = ahead(x, d, 4)
+        return remote(
+            second_part.at[at], second_in2.at[d - 1], p2y_send.at[d - 1], p2y_recv.at[d - 1],
+            device(z, y, at, core),
+        )
+
+    for d in (2, 1, 3):
+        p2x_copy(d).start()
+    for u in range(2):
+        for d in range(1, 4):
+            remote(
+                second_sum.at[0], second_in.at[d - 1, u], p1y_send.at[0], p1y_recv.at[d - 1, u],
+                device(z, ahead(y, d, 4), x, core),
+            ).wait_recv()
+        j = 4 * u + 2 * y_lo + y_hi
+        total = second_sum[j] + second_in[0, u] + second_in[1, u] + second_in[2, u]
+        second_part[2 * u] = total[:64]
+        second_part[2 * u + 1] = total[64:]
+    for d in (2, 1, 3):
+        p2y_copy(d).start()
+
+    for d in range(1, 4):
+        p2x_copy(d).wait_recv()
+    total = first_part[y] + first_in2[0] + first_in2[1] + first_in2[2]
+    slab[:, 0:8, :] = total[:64].reshape(8, 8, HALF)
+    slab[:, 8:16, :] = jnp.broadcast_to(total[64:][None], (8, 8, HALF))
+    for d in range(1, 4):
+        p2y_copy(d).wait_recv()
+    total = second_part[x] + second_in2[0] + second_in2[1] + second_in2[2]
+    slab[:, 16:24, :] = total.reshape(8, 8, HALF)
+
+    def z_copy(d):
+        at = ahead(z, d, depth)
+        return remote(
+            slab.at[at], slab_in.at[d - 1], z_send.at[d - 1], z_recv.at[d - 1],
+            device(at, y, x, core),
+        )
+
+    order = (4, 3, 5, 2, 6, 1, 7)
+    for d in order:
+        z_copy(d).start()
+    for d in order:
+        z_copy(d).wait_recv()
+    total = slab[z]
+    for d in range(1, depth):
+        total = total + slab_in[d - 1]
+    final[...] = total
+
+    def gx_copy(d):
+        at = ahead(z, d, depth)
+        return remote(
+            final.at[0:16], first_all.at[y_lo, z], gx_send.at[d], gx_recv.at[y_lo, z],
+            device(at, 2 * y_hi + x_lo, x, core),
+        )
+
+    def gy_copy(d):
+        at = ahead(z, d, depth)
+        return remote(
+            final.at[16:24], second_all.at[x_lo, z], gy_send.at[d], gy_recv.at[x_lo, z],
+            device(at, y, 2 * x_hi + y_lo, core),
+        )
+
+    for d in order:
+        gx_copy(d).start()
+        gy_copy(d).start()
+
+    @pl.when(jnp.logical_not(solver))
+    def _():
+        gx_copy(0).start()
+        gy_copy(0).start()
+
+    def w_copy(k):
+        to = plane(*in_plane[k])
+        return remote(coef, coefs.at[8 * core + 2 * x + y_hi], w_send.at[k],
+                      w_recv.at[8 * core + 2 * x + y_hi], to)
+
+    @pl.when(solver)
+    def _():
+        pltpu.make_async_copy(final.at[0:16], first_all.at[y_lo, z], gx_recv.at[y_lo, z]).start()
+        pltpu.make_async_copy(final.at[16:24], second_all.at[x_lo, z], gy_recv.at[x_lo, z]).start()
+        for s in range(2):
+            for k in range(8):
+                remote(final.at[0:16], first_all.at[s, k], gx_send.at[0], gx_recv.at[s, k],
+                       plane(0, 0, 1)).wait_recv()
+                remote(final.at[16:24], second_all.at[s, k], gy_send.at[0], gy_recv.at[s, k],
+                       plane(0, 0, 1)).wait_recv()
+        mixed = first_all[:, :, 0:8, :].reshape(HALF, HALF)
+        extra = first_all[0, 0, 8:16, :]
+        low = second_all[...].reshape(HALF, HALF)
+        coef[...] = solved(mixed, extra, low)
+        for k in range(len(in_plane)):
+            w_copy(k).start()
+        mine = 8 * core + 2 * x + y_hi
+        pltpu.make_async_copy(coef, coefs.at[mine], w_recv.at[mine]).start()
+
+    for k in range(LEAVES):
+        remote(coef, coefs.at[k], w_send.at[0], w_recv.at[k], plane(0, 0, 1)).wait_recv()
+    block = coefs[...]
+    weights = jnp.concatenate([block[:, 0, :], block[:, 1, :]], axis=1)
+    leaf_output(features, leaf, score, weights, block[:, 2, :], out.at[1], out.at[2])
+
+    def sent(t, carry):
+        j = turn(t)
+        pair_copy(j).wait_send()
+
+        @pl.when(t < 6)
+        def _():
+            p1x_copy(t).wait_send()
+
+        @pl.when(row_of(j) != y)
+        def _():
+            p1y_copy(j).wait_send()
+
+        return carry
+
+    lax.fori_loop(0, 8, sent, 0)
+    for d in range(1, 4):
+        p2x_copy(d).wait_send()
+        p2y_copy(d).wait_send()
+    for d in range(1, depth):
+        z_copy(d).wait_send()
+        gx_copy(d).wait_send()
+        gy_copy(d).wait_send()
+
+    @pl.when(jnp.logical_not(solver))
+    def _():
+        gx_copy(0).wait_send()
+        gy_copy(0).wait_send()
+
+    @pl.when(solver)
+    def _():
+        for k in range(len(in_plane)):
+            w_copy(k).wait_send()
 
 
 def body(features, scores, labels, query_ids, ranks, leaf_ids):
     lines = [x.reshape(BLOCKS, MAXQ) for x in (scores, labels, query_ids, ranks, leaf_ids)]
-    score, label, query, rank, leaf = lines
-    info = jnp.stack([x.astype(F32) for x in (query, label, rank, score)])
-    index = lax.axis_index(DOC_LEAF)
-    before = passed_along(info[:, BLOCKS - 1], DOC_LEAF, 1)
-    after = passed_along(info[:, 0], DOC_LEAF, -1)
-    none = jnp.full((1, MAXQ), -1.0, F32)
-    before = jnp.where((index == 0) & (jnp.arange(4)[:, None] == 0), none, before)
-    after = jnp.where(
-        (index == lax.axis_size(DOC_LEAF) - 1) & (jnp.arange(4)[:, None] == 0), none, after
-    )
-    grads, packed = pl.pallas_call(
-        terms_kernel,
-        out_shape=[
-            jax.ShapeDtypeStruct((BLOCKS, MAXQ), F32),
-            jax.ShapeDtypeStruct((LEAVES, LEAF_ROWS, HALF), F32),
-        ],
-        in_specs=[VMEM] * 8,
-        out_specs=[VMEM] * 2,
+    dma = pltpu.SemaphoreType.DMA
+    tile = lambda *shape: pltpu.VMEM((*shape, HALF), F32)
+    out = pl.pallas_call(
+        level_kernel,
+        out_shape=jax.ShapeDtypeStruct((3, BLOCKS, MAXQ), F32),
+        in_specs=[VMEM] * 6,
+        out_specs=VMEM,
         scratch_shapes=[
             pltpu.VMEM((F, ROWS), BF16),
             pltpu.VMEM((LEAVES, ROWS), F32),
-            pltpu.VMEM((6, LEAVES, MAXQ), F32),
+            tile(6, LEAVES),
+            tile(2, 8), tile(8), tile(8),
+            tile(8, LEAF_ROWS), tile(8, LEAF_ROWS),
+            tile(8, 144), tile(8, 128), tile(3, 2, 144), tile(3, 2, 128),
+            tile(4, 72), tile(4, 64), tile(3, 72), tile(3, 64),
+            tile(8, 24), tile(7, 24), tile(24), tile(2, 8, 16), tile(2, 8, 8), tile(8),
+            tile(LEAVES, 8),
+            dma((2,)), dma((2,)), dma((8,)), dma((8,)),
+            dma((8,)), dma((3, 2)), dma((8,)), dma((3, 2)),
+            dma((3,)), dma((3,)), dma((3,)), dma((3,)),
+            dma((7,)), dma((7,)), dma((8,)), dma((2, 8)), dma((8,)), dma((2, 8)),
+            dma((31,)), dma((LEAVES,)),
         ],
-    )(features, score, label, query, rank, leaf, before, after)
-    part = lax.psum_scatter(packed, LEAF, scatter_dimension=0, tiled=False)
-    total = lax.psum(part, "doc")
-    coefs = pl.pallas_call(
-        solve_kernel,
-        out_shape=jax.ShapeDtypeStruct((8, HALF), F32),
-        in_specs=[VMEM],
-        out_specs=VMEM,
-    )(total)
-    gathered = lax.all_gather(coefs, LEAF, axis=1)
-    tree, new = pl.pallas_call(
-        output_kernel,
-        out_shape=[jax.ShapeDtypeStruct((BLOCKS, MAXQ), F32)] * 2,
-        in_specs=[VMEM] * 4,
-        out_specs=[VMEM] * 2,
-    )(features, leaf, score, gathered)
-    return grads.reshape(ROWS), tree.reshape(ROWS), new.reshape(ROWS)
+        compiler_params=pltpu.CompilerParams(collective_id=0, has_side_effects=True),
+    )(features, *lines)
+    return out[0].reshape(ROWS), out[1].reshape(ROWS), out[2].reshape(ROWS)
 
 
 def solution(mesh):
-    torus = Mesh(
-        mesh.devices.reshape(mesh.shape["doc"], 4, 2, 2), ("doc", "leaf_0", "leaf_1", "leaf_2")
-    )
-    spec = P(DOC_LEAF)
+    torus = Mesh(mesh.devices.reshape(mesh.shape["doc"] // 2, 2, 4, 2, 2), AXES)
+    spec = P(AXES)
     return jax.shard_map(
         body,
         mesh=torus,
-        in_specs=(P(DOC_LEAF, None), spec, spec, spec, spec, spec),
+        in_specs=(P(AXES, None), spec, spec, spec, spec, spec),
         out_specs=(spec, spec, spec),
         check_vma=False,
     )

time: 292 us -> 67.4 us (0.23)
  waiting for transfers between devices: 208 us -> 0 us
  Pallas kernels: 24 us -> 65.3 us
  blocking collectives: 35.9 us -> 0 us
  between operations: 14 us -> 0.64 us
  starting transfers between devices: 4.72 us -> 0 us
  other arithmetic: 4.06 us -> 0 us
    psum x1 -> x0, waiting for transfers between devices: 125 us -> none  [body(): total = lax.psum(part, 'doc')]
    reduce_scatter x1 -> x0, waiting for transfers between devices: 76.8 us -> none  [body(): part = lax.psum_scatter(packed, LEAF, scatter_dimension=0, tiled=False)]
    pallas_call x3 -> x1, Pallas kernels: 24 us -> 65.3 us  [body(): pl.pallas_call(level_kernel, out_shape=jax.ShapeDtypeStruct((3, BLOCKS, M...]
    all_gather x1 -> x0, blocking collectives: 35.9 us -> none  [body(): gathered = lax.all_gather(coefs, LEAF, axis=1)]
    ppermute x2 -> x0, waiting for transfers between devices: 7.04 us -> none  [passed_along(): lax.ppermute(value, axis, [(i, (i + by) % devices) for i in range(devices)])]
    ppermute x2 -> x0, starting transfers between devices: 4.46 us -> none  [passed_along(): lax.ppermute(value, axis, [(i, (i + by) % devices) for i in range(devices)])]
  transfers between devices with their start and end apart: 4 -> 0, of which waited for: 4 -> 0; matrix products, arithmetic and copies ran while one was open for 0% -> 0% of each run, Pallas kernels for 0% -> 0%
where the time goes in v2:
time: 67.4 us; the launch traced here: 67.2 us
  Pallas kernels  65.3 us (97%)
  local copies, waits for them, and re-layouts  1.29 us (2%)
    pallas_call x1, Pallas kernels, body(): pl.pallas_call(level_kernel, out_shape=jax.ShapeDtypeStruct((3, BLOCKS, M...  65.3 us

profile of v2, /device:TPU:1, one launch (start us, length us, event | category | flops | bytes accessed | tf_op | source)
XLA Modules:
  0.0 67.2 jit_solution(626906716860091697)
XLA Ops:
  0.6 65.3 %shard_map.85 = f32[3,8,128]{2,1,0:T(8,128)} custom-call(bf16[1024,256]{1,0:T(8,128)(2,1)} %features.1, f32[8,128]{1,0:T(8,128)} %bitcast.11, s32[8,128]{1,0:T(8,128)} %bitcast.12, s32[8,128]{1,0:T(8,128)} %bitcast.13, s32[8,128]{1,0:T(8,128)} %bitcast.14, s32[8,128]{1,0:T(8,128)} %bitcast.15), custom_call_target="tpu_custom_call" | custom-call | tf_op jit(solution)/shard_map/pallas_call | solution.py:605
  65.9 1.3 %slice_bitcast_fusion = (f32[1024]{0:T(1024)}, f32[1024]{0:T(1024)}, f32[1024]{0:T(1024)}) fusion(f32[3,8,128]{2,1,0:T(8,128)} %shard_map.85), kind=kLoop, calls=%fused_computation | loop fusion | bytes 24576 | tf_op jit(solution)/shard_map/reshape;squeeze | solution.py:628

commit v3 on v2

--- a/solution.py
+++ b/solution.py
@@ -15,7 +15,10 @@
 LEAF_ROWS = 272
 AXES = ("z", "y_lo", "x", "y_hi", "core")
 MESH = pl.DeviceIdType.MESH
-PIVOTS = 4
+PIVOTS = 8
+INNER = slice(MAXQ, ROWS - MAXQ)
+DEEP = ROWS - 2 * MAXQ
+EDGE = 2 * MAXQ
 LAMBDA = 1.0
 SHRINKAGE = 0.1
 F32 = jnp.float32
@@ -97,77 +100,66 @@
 
 
 def normalized(sums):
+    pull, push, counts = sums
     position = (iota((MAXQ, MAXQ), 0) + 1).astype(F32)
     disc_at = discount(position)
-    grads, hess = [], []
-    for pull, push, counts in sums:
-        ideal = jnp.zeros((1, MAXQ), F32)
-        for level in range(4):
-            inside = jnp.where(position <= counts[level : level + 1, :], disc_at, 0.0)
-            ideal = ideal + float(2**level) * jnp.sum(inside, axis=0, keepdims=True)
-        inverse = 1.0 / jnp.maximum(ideal, 1.0)
-        grads.append(-inverse * pull)
-        hess.append(inverse * push)
-    return grads, hess
-
-
-def leaf_inputs(features_ref, leaf_ref, grads, hess, weighted_ref, in_leaf_ref, sums_ref):
+    ideal = jnp.zeros((1, MAXQ), F32)
+    for level in range(4):
+        inside = jnp.where(position <= counts[level : level + 1, :], disc_at, 0.0)
+        ideal = ideal + float(2**level) * jnp.sum(inside, axis=0, keepdims=True)
+    inverse = 1.0 / jnp.maximum(ideal, 1.0)
+    return -inverse * pull, inverse * push
+
+
+def leaf_masks(leaf_ref, blocks):
     leaf = leaf_ref[...]
-    grad_low = []
-    h_lanes = jnp.zeros((LEAVES, MAXQ), F32)
-    g_lanes = jnp.zeros((LEAVES, MAXQ), F32)
-    for k in range(BLOCKS):
-        rows = slice(MAXQ * k, MAXQ * (k + 1))
-        turned = features_ref[rows, :].astype(F32).T
-        weighted_ref[:, rows] = (turned * hess[k]).astype(BF16)
-        in_leaf = jnp.where(
-            jnp.broadcast_to(leaf[k : k + 1, :], (LEAVES, MAXQ)) == iota((LEAVES, MAXQ), 0),
-            1.0,
-            0.0,
-        )
-        in_leaf_ref[:, rows] = in_leaf
-        h_lanes = h_lanes + in_leaf * hess[k]
-        g_lanes = g_lanes + in_leaf * grads[k]
-        grad_low.append((in_leaf * grads[k]).astype(BF16))
-    moment = jnp.dot(
-        jnp.concatenate(grad_low, axis=1), features_ref[...], preferred_element_type=F32
+    wide = (LEAVES, MAXQ)
+    return [
+        jnp.where(jnp.broadcast_to(leaf[k : k + 1, :], wide) == iota(wide, 0), 1.0, 0.0)
+        for k in blocks
+    ]
+
+
+def leaf_sums(in_leaf, grads, hess, features, weighted):
+    total = lambda parts: jnp.broadcast_to(
+        jnp.sum(tree_sum(parts), axis=1, keepdims=True), (LEAVES, MAXQ)
     )
-    hsum = lax.dot_general(
-        in_leaf_ref[...].astype(BF16), weighted_ref[...], NT, preferred_element_type=F32
-    )
-    wide = (LEAVES, MAXQ)
-    sums_ref[0] = hsum[:, :HALF]
-    sums_ref[1] = hsum[:, HALF:]
-    sums_ref[2] = moment[:, :HALF]
-    sums_ref[3] = moment[:, HALF:]
-    sums_ref[4] = jnp.broadcast_to(jnp.sum(h_lanes, axis=1, keepdims=True), wide)
-    sums_ref[5] = jnp.broadcast_to(jnp.sum(g_lanes, axis=1, keepdims=True), wide)
-
-
-def leaf_gram(number, features_ref, weighted_ref, in_leaf_ref):
-    mask = jnp.broadcast_to(in_leaf_ref[pl.ds(number, 1), :], (16, ROWS)).astype(BF16)
-    own = (weighted_ref[...].reshape(16, 16, ROWS) * mask[None]).reshape(F, ROWS)
-    return jnp.dot(own, features_ref[...], preferred_element_type=F32)
-
-
-def packed_leaf(gram, number, sums_ref):
+    low = jnp.concatenate([(m * g).astype(BF16) for m, g in zip(in_leaf, grads)], axis=1)
+    moment = jnp.dot(low, features, preferred_element_type=F32)
+    masks = jnp.concatenate([m.astype(BF16) for m in in_leaf], axis=1)
+    hsum = lax.dot_general(masks, weighted, NT, preferred_element_type=F32)
+    return [
+        hsum[:, :HALF],
+        hsum[:, HALF:],
+        moment[:, :HALF],
+        moment[:, HALF:],
+        total([m * h for m, h in zip(in_leaf, hess)]),
+        total([m * g for m, g in zip(in_leaf, grads)]),
+    ]
+
+
+def leaf_gram(mask, features, weighted):
+    n = features.shape[0]
+    own = (weighted.reshape(16, 16, n) * jnp.broadcast_to(mask, (16, n)).astype(BF16)[None])
+    gram = jnp.dot(own.reshape(F, n), features, preferred_element_type=F32)
     row = iota((HALF, HALF), 0)
     col = iota((HALF, HALF), 1)
     last = gram[HALF:, HALF:]
     mixed = jnp.where(col <= row, gram[:HALF, :HALF], last)
     diag = jnp.sum(jnp.where(col == row, last, 0.0), axis=0, keepdims=True)
-    small = [sums_ref[k, pl.ds(number, 1), :] for k in range(6)]
-    extra = stacked(small + [diag])
-    first = jnp.concatenate(
-        [mixed[:64], extra, mixed[64:], jnp.zeros((8, HALF), F32)], axis=0
-    )
-    return first, gram[HALF:, :HALF]
+    return mixed, diag, gram[HALF:, :HALF]
 
 
 def dotted(a, b, dims=(((1,), (0,)), ((), ()))):
     return lax.dot_general(
         a, b, dims, precision=lax.Precision.HIGHEST, preferred_element_type=F32
     )
+
+
+def tree_sum(terms):
+    while len(terms) > 1:
+        terms = [sum(terms[k : k + 2][1:], terms[k]) for k in range(0, len(terms), 2)]
+    return terms[0]
 
 
 def small_inverse(d):
@@ -182,10 +174,7 @@
     h = p // 2
 
     def dot(xs, ys):
-        total = xs[0] * ys[0]
-        for x, y in zip(xs[1:], ys[1:]):
-            total = total + x * y
-        return total
+        return tree_sum([x * y for x, y in zip(xs, ys)])
 
     first = small_inverse([line[:h] for line in d[:h]])
     side = [line[h:] for line in d[:h]]
@@ -225,23 +214,20 @@
         v = small_inverse(d)
         scaled = []
         for a in range(p):
-            r = v[a][0] * rows[0]
-            for b in range(1, p):
-                r = r + v[a][b] * rows[b]
+            r = tree_sum([v[a][b] * rows[b] for b in range(p)])
             for b in range(p):
                 r = jnp.where(lane == k + b, v[a][b], r)
             scaled.append(r)
         pivot = (lane >= k) & (lane < k + p)
-        whole = jnp.where(jnp.broadcast_to(pivot[:1], m.shape), 0.0, m)
-        for a in range(p):
-            whole = whole - cols[a] * jnp.broadcast_to(scaled[a][:1], m.shape)
-        tile = whole[top : top + 8]
-        for a in range(p):
-            tile = jnp.where(sub == k - top + a, scaled[a], tile)
-        parts = [whole[:top]] if top else []
-        parts += [tile]
-        parts += [whole[top + 8 :]] if top + 8 < n else []
-        m = jnp.concatenate(parts, axis=0)
+        tiles = {}
+        for t in [(k + p) // 8 * 8 % n] + [t for t in range(0, n, 8) if t != (k + p) // 8 * 8 % n]:
+            tile = jnp.where(pivot, 0.0, m[t : t + 8, :])
+            tile = tile - tree_sum([cols[a][t : t + 8, :] * scaled[a] for a in range(p)])
+            if t == top:
+                for a in range(p):
+                    tile = jnp.where(sub == k - top + a, scaled[a], tile)
+            tiles[t] = tile
+        m = jnp.concatenate([tiles[t] for t in range(0, n, 8)], axis=0)
     return m
 
 
@@ -323,7 +309,8 @@
 def level_kernel(
     features, score, label, query, rank, leaf,
     out,
-    weighted, in_leaf, sums_ref,
+    inner_weighted, edge_turned, edge_weighted, edge_features, in_leaf, sums_ref,
+    inner_mixed, inner_diag, inner_low,
     edge, before, after,
     pair_out, pair_in,
     first_sum, second_sum, first_in, second_in,
@@ -366,6 +353,42 @@
     edge[0] = stacked([r[BLOCKS - 1 : BLOCKS, :] for r in rows])
     edge[1] = stacked([r[0:1, :] for r in rows])
     own, sums = lambdas_within(rows)
+
+    inner = range(1, BLOCKS - 1)
+    ends = (0, BLOCKS - 1)
+    grads, hess = {}, {}
+    for b in range(BLOCKS):
+        turned = features[MAXQ * b : MAXQ * (b + 1), :].astype(F32).T
+        if b in inner:
+            grads[b], hess[b] = normalized(sums[b])
+            out[0, b : b + 1, :] = grads[b]
+            inner_weighted[:, MAXQ * (b - 1) : MAXQ * b] = (turned * hess[b]).astype(BF16)
+        else:
+            place = MAXQ * ends.index(b)
+            edge_turned[:, place : place + MAXQ] = turned.astype(BF16)
+            edge_features[place : place + MAXQ, :] = features[MAXQ * b : MAXQ * (b + 1), :]
+    masks = leaf_masks(leaf, inner)
+    for b in inner:
+        in_leaf[:, MAXQ * (b - 1) : MAXQ * b] = masks[b - 1]
+    end_masks = leaf_masks(leaf, ends)
+    in_leaf[:, DEEP : DEEP + MAXQ] = end_masks[0]
+    in_leaf[:, DEEP + MAXQ :] = end_masks[1]
+    small = leaf_sums(
+        masks, [grads[b] for b in inner], [hess[b] for b in inner], features[INNER, :], inner_weighted[...]
+    )
+    for k in range(6):
+        sums_ref[k] = small[k]
+
+    def inner_leaf(number, carry):
+        mixed, diag, low = leaf_gram(
+            in_leaf[pl.ds(number, 1), :DEEP], features[INNER, :], inner_weighted[...]
+        )
+        inner_mixed[number] = mixed
+        inner_diag[number] = jnp.broadcast_to(diag, (8, HALF))
+        inner_low[number] = low
+        return carry
+
+    lax.fori_loop(0, LEAVES, inner_leaf, 0)
     pl.semaphore_wait(barrier, len(partners))
 
     later, earlier = neighbour(1), neighbour(-1)
@@ -381,10 +404,29 @@
     was = jnp.where(top & first_device, -1.0, before[...])
     will = jnp.where(top & last_device, -1.0, after[...])
     lambdas_across(own, sums, was, will)
-    grads, hess = normalized(sums)
-    for k in range(BLOCKS):
-        out[0, k : k + 1, :] = grads[k]
-    leaf_inputs(features, leaf, grads, hess, weighted, in_leaf, sums_ref)
+    for b in ends:
+        grads[b], hess[b] = normalized(sums[b])
+        out[0, b : b + 1, :] = grads[b]
+        place = MAXQ * ends.index(b)
+        turned = edge_turned[:, place : place + MAXQ].astype(F32)
+        edge_weighted[:, place : place + MAXQ] = (turned * hess[b]).astype(BF16)
+    small = leaf_sums(
+        end_masks, [grads[b] for b in ends], [hess[b] for b in ends], edge_features[...], edge_weighted[...]
+    )
+    for k in range(6):
+        sums_ref[k] = sums_ref[k] + small[k]
+
+    def packed_leaf(number):
+        mixed, diag, low = leaf_gram(
+            in_leaf[pl.ds(number, 1), DEEP:], edge_features[...], edge_weighted[...]
+        )
+        mixed = mixed + inner_mixed[number]
+        extra = [sums_ref[k, pl.ds(number, 1), :] for k in range(6)]
+        extra = stacked(extra + [diag + inner_diag[number, 0:1, :]])
+        first = jnp.concatenate(
+            [mixed[:64], extra, mixed[64:], jnp.zeros((8, HALF), F32)], axis=0
+        )
+        return first, low + inner_low[number]
 
     def turn(t):
         return lax.rem(2 * (x + 1) + t, 8)
@@ -397,7 +439,7 @@
     def for_other(t, carry):
         j = turn(t)
         number = 8 * other + j
-        first, second = packed_leaf(leaf_gram(number, features, weighted, in_leaf), number, sums_ref)
+        first, second = packed_leaf(number)
         pair_out[j, :144, :] = first
         pair_out[j, 144:, :] = second
         pair_copy(j).start()
@@ -431,7 +473,7 @@
     def for_own(t, carry):
         j = turn(t)
         number = 8 * core + j
-        first, second = packed_leaf(leaf_gram(number, features, weighted, in_leaf), number, sums_ref)
+        first, second = packed_leaf(number)
         pair_copy(j).wait_recv()
         first_sum[j] = first + pair_in[j, :144, :]
         second_sum[j] = second + pair_in[j, 144:, :]
@@ -608,9 +650,13 @@
         in_specs=[VMEM] * 6,
         out_specs=VMEM,
         scratch_shapes=[
-            pltpu.VMEM((F, ROWS), BF16),
+            pltpu.VMEM((F, DEEP), BF16),
+            pltpu.VMEM((F, EDGE), BF16),
+            pltpu.VMEM((F, EDGE), BF16),
+            pltpu.VMEM((EDGE, F), BF16),
             pltpu.VMEM((LEAVES, ROWS), F32),
             tile(6, LEAVES),
+            tile(LEAVES, HALF), tile(LEAVES, 8), tile(LEAVES, HALF),
             tile(2, 8), tile(8), tile(8),
             tile(8, LEAF_ROWS), tile(8, LEAF_ROWS),
             tile(8, 144), tile(8, 128), tile(3, 2, 144), tile(3, 2, 128),

time: 67.4 us -> 65.9 us (0.978)
  Pallas kernels: 65.3 us -> 63.8 us
    pallas_call x1, Pallas kernels: 65.3 us -> 63.8 us  [body(): pl.pallas_call(level_kernel, out_shape=jax.ShapeDtypeStruct((3, BLOCKS, M...]
where the time goes in v3:
time: 65.9 us; the launch traced here: 65.8 us
  Pallas kernels  63.8 us (97%)
  local copies, waits for them, and re-layouts  1.29 us (2%)
    pallas_call x1, Pallas kernels, body(): pl.pallas_call(level_kernel, out_shape=jax.ShapeDtypeStruct((3, BLOCKS, M...  63.8 us

profile of v3, /device:TPU:1, one launch (start us, length us, event | category | flops | bytes accessed | tf_op | source)
XLA Modules:
  0.0 65.8 jit_solution(3223624784868221821)
XLA Ops:
  0.6 63.8 %shard_map.85 = f32[3,8,128]{2,1,0:T(8,128)} custom-call(bf16[1024,256]{1,0:T(8,128)(2,1)} %features.1, f32[8,128]{1,0:T(8,128)} %bitcast.11, s32[8,128]{1,0:T(8,128)} %bitcast.12, s32[8,128]{1,0:T(8,128)} %bitcast.13, s32[8,128]{1,0:T(8,128)} %bitcast.14, s32[8,128]{1,0:T(8,128)} %bitcast.15), custom_call_target="tpu_custom_call" | custom-call | tf_op jit(solution)/shard_map/pallas_call | solution.py:647
  64.5 1.3 %slice_bitcast_fusion = (f32[1024]{0:T(1024)}, f32[1024]{0:T(1024)}, f32[1024]{0:T(1024)}) fusion(f32[3,8,128]{2,1,0:T(8,128)} %shard_map.85), kind=kLoop, calls=%fused_computation | loop fusion | bytes 24576 | tf_op jit(solution)/shard_map/reshape;squeeze | solution.py:674

commit v4 on v3

--- a/solution.py
+++ b/solution.py
@@ -94,9 +94,8 @@
     return own, sums
 
 
-def lambdas_across(own, sums, before, after):
-    meet(own, sums, 0, far_block(*[before[c : c + 1, :] for c in range(4)]))
-    meet(own, sums, BLOCKS - 1, far_block(*[after[c : c + 1, :] for c in range(4)]))
+def added(first, second):
+    return tuple(a + b for a, b in zip(first, second))
 
 
 def normalized(sums):
@@ -111,13 +110,9 @@
     return -inverse * pull, inverse * push
 
 
-def leaf_masks(leaf_ref, blocks):
-    leaf = leaf_ref[...]
+def leaf_mask(leaf):
     wide = (LEAVES, MAXQ)
-    return [
-        jnp.where(jnp.broadcast_to(leaf[k : k + 1, :], wide) == iota(wide, 0), 1.0, 0.0)
-        for k in blocks
-    ]
+    return jnp.where(jnp.broadcast_to(leaf, wide) == iota(wide, 0).astype(F32), 1.0, 0.0)
 
 
 def leaf_sums(in_leaf, grads, hess, features, weighted):
@@ -309,14 +304,14 @@
 def level_kernel(
     features, score, label, query, rank, leaf,
     out,
-    inner_weighted, edge_turned, edge_weighted, edge_features, in_leaf, sums_ref,
+    inner_weighted, outer_turned, outer_weighted, outer_features, in_leaf, sums_ref, end_sums,
     inner_mixed, inner_diag, inner_low,
-    edge, before, after,
+    edge, halo, info, info_in, outer_out, outer_in,
     pair_out, pair_in,
     first_sum, second_sum, first_in, second_in,
     first_part, second_part, first_in2, second_in2,
     slab, slab_in, final, first_all, second_all, coef, coefs,
-    halo_send, halo_recv, pair_send, pair_recv,
+    halo_send, halo_recv, mate_send, mate_recv, pair_send, pair_recv,
     p1x_send, p1x_recv, p1y_send, p1y_recv,
     p2x_send, p2x_recv, p2y_send, p2y_recv,
     z_send, z_recv, gx_send, gx_recv, gy_send, gy_recv,
@@ -336,8 +331,11 @@
     def plane(dx, dy, dc):
         return device(z, ahead(y, dy, 4), ahead(x, dx, 4), ahead(core, dc, 2))
 
+    def pick(a, b):
+        return jnp.where(core == 0, a, b)
+
     barrier = pltpu.get_barrier_semaphore()
-    partners = [neighbour(1), neighbour(-1)] + [plane(*d) for d in in_plane]
+    partners = [neighbour(by - core) for by in (-2, -1, 2, 3)] + [plane(*d) for d in in_plane]
     for d in range(1, depth):
         at = ahead(z, d, depth)
         partners += [device(at, y, x, core), device(at, y_pair, x, core), device(at, y, x_pair, core)]
@@ -350,34 +348,36 @@
         )
 
     rows = own_rows(query, label, rank, score)
+    leaves = leaf[...].astype(F32)
     edge[0] = stacked([r[BLOCKS - 1 : BLOCKS, :] for r in rows])
     edge[1] = stacked([r[0:1, :] for r in rows])
+    for k in range(4):
+        info[k] = rows[k]
+    info[4] = leaves
+    outer_start = pl.multiple_of(core * (ROWS - MAXQ), MAXQ)
+    middle_start = pl.multiple_of(other * (ROWS - MAXQ), MAXQ)
+    outer_out[...] = features[pl.ds(outer_start, MAXQ), :].astype(F32)
     own, sums = lambdas_within(rows)
 
     inner = range(1, BLOCKS - 1)
-    ends = (0, BLOCKS - 1)
-    grads, hess = {}, {}
-    for b in range(BLOCKS):
+    grads, hess = [], []
+    for b in inner:
         turned = features[MAXQ * b : MAXQ * (b + 1), :].astype(F32).T
-        if b in inner:
-            grads[b], hess[b] = normalized(sums[b])
-            out[0, b : b + 1, :] = grads[b]
-            inner_weighted[:, MAXQ * (b - 1) : MAXQ * b] = (turned * hess[b]).astype(BF16)
-        else:
-            place = MAXQ * ends.index(b)
-            edge_turned[:, place : place + MAXQ] = turned.astype(BF16)
-            edge_features[place : place + MAXQ, :] = features[MAXQ * b : MAXQ * (b + 1), :]
-    masks = leaf_masks(leaf, inner)
+        g, h = normalized(sums[b])
+        grads.append(g)
+        hess.append(h)
+        out[0, b : b + 1, :] = g
+        inner_weighted[:, MAXQ * (b - 1) : MAXQ * b] = (turned * h).astype(BF16)
+    masks = [leaf_mask(leaves[b : b + 1, :]) for b in inner]
     for b in inner:
         in_leaf[:, MAXQ * (b - 1) : MAXQ * b] = masks[b - 1]
-    end_masks = leaf_masks(leaf, ends)
-    in_leaf[:, DEEP : DEEP + MAXQ] = end_masks[0]
-    in_leaf[:, DEEP + MAXQ :] = end_masks[1]
-    small = leaf_sums(
-        masks, [grads[b] for b in inner], [hess[b] for b in inner], features[INNER, :], inner_weighted[...]
-    )
+    small = leaf_sums(masks, grads, hess, features[INNER, :], inner_weighted[...])
     for k in range(6):
         sums_ref[k] = small[k]
+    middle_turned = outer_weighted.at[:, :MAXQ]
+    middle_turned[...] = features[pl.ds(middle_start, MAXQ), :].astype(F32).T.astype(BF16)
+    outer_turned[:, :MAXQ] = outer_out[...].T.astype(BF16)
+    outer_features[:MAXQ, :] = features[pl.ds(outer_start, MAXQ), :]
 
     def inner_leaf(number, carry):
         mixed, diag, low = leaf_gram(
@@ -391,34 +391,41 @@
     lax.fori_loop(0, LEAVES, inner_leaf, 0)
     pl.semaphore_wait(barrier, len(partners))
 
-    later, earlier = neighbour(1), neighbour(-1)
-    to_later = remote(edge.at[0], before, halo_send.at[0], halo_recv.at[0], later)
-    to_earlier = remote(edge.at[1], after, halo_send.at[1], halo_recv.at[1], earlier)
-    to_later.start()
-    to_earlier.start()
-    to_later.wait()
-    to_earlier.wait()
-    first_device = (z == 0) & (y_lo == 0) & (x == 0) & (y_hi == 0) & (core == 0)
-    last_device = (z == depth - 1) & (y_lo == 1) & (x == 3) & (y_hi == 1) & (core == 1)
-    top = iota((8, MAXQ), 0) == 0
-    was = jnp.where(top & first_device, -1.0, before[...])
-    will = jnp.where(top & last_device, -1.0, after[...])
-    lambdas_across(own, sums, was, will)
-    for b in ends:
-        grads[b], hess[b] = normalized(sums[b])
-        out[0, b : b + 1, :] = grads[b]
-        place = MAXQ * ends.index(b)
-        turned = edge_turned[:, place : place + MAXQ].astype(F32)
-        edge_weighted[:, place : place + MAXQ] = (turned * hess[b]).astype(BF16)
-    small = leaf_sums(
-        end_masks, [grads[b] for b in ends], [hess[b] for b in ends], edge_features[...], edge_weighted[...]
-    )
+    halos = [
+        remote(
+            edge.at[other], halo.at[other], halo_send.at[k], halo_recv.at[other],
+            neighbour(pick(-2, 1) + k),
+        )
+        for k in range(2)
+    ]
+    for copy in halos:
+        copy.start()
+    info_copy = remote(info, info_in, mate_send.at[0], mate_recv.at[0], plane(0, 0, 1))
+    outer_copy = remote(outer_out, outer_in, mate_send.at[1], mate_recv.at[1], plane(0, 0, 1))
+    info_copy.start()
+    outer_copy.start()
+    info_copy.wait_recv()
+
+    mate = [info_in[k] for k in range(4)]
+    beside = far_block(*[pick(r[:1], r[BLOCKS - 1 :]) for r in mate])
+    middle = [pick(r[BLOCKS - 1 :], r[:1]) for r in own]
+    middle_sums = tuple(pick(a, b) for a, b in zip(sums[BLOCKS - 1], sums[0]))
+    g, h = normalized(added(middle_sums, pair_sums(middle, *beside)))
+    out[0, pl.ds(other * (BLOCKS - 1), 1), :] = g
+    middle_weighted = (middle_turned[...].astype(F32) * h).astype(BF16)
+    middle_mask = leaf_mask(pick(leaves[BLOCKS - 1 :], leaves[:1]))
+    middle_features = features[pl.ds(middle_start, MAXQ), :]
+    in_leaf[:, DEEP : DEEP + MAXQ] = middle_mask
+    small = leaf_sums([middle_mask], [g], [h], middle_features, middle_weighted)
     for k in range(6):
         sums_ref[k] = sums_ref[k] + small[k]
-
-    def packed_leaf(number):
+    outer_weighted[:, :MAXQ] = middle_weighted
+
+    def chip_leaf(number):
         mixed, diag, low = leaf_gram(
-            in_leaf[pl.ds(number, 1), DEEP:], edge_features[...], edge_weighted[...]
+            in_leaf[pl.ds(number, 1), DEEP : DEEP + 2 * MAXQ][:, :MAXQ],
+            features[pl.ds(middle_start, MAXQ), :],
+            outer_weighted[:, :MAXQ],
         )
         mixed = mixed + inner_mixed[number]
         extra = [sums_ref[k, pl.ds(number, 1), :] for k in range(6)]
@@ -438,14 +445,73 @@
 
     def for_other(t, carry):
         j = turn(t)
-        number = 8 * other + j
-        first, second = packed_leaf(number)
+        first, second = chip_leaf(8 * other + j)
         pair_out[j, :144, :] = first
         pair_out[j, 144:, :] = second
         pair_copy(j).start()
         return carry
 
     lax.fori_loop(0, 8, for_other, 0)
+
+    def for_own_rows(t, carry):
+        j = turn(t)
+        first, second = chip_leaf(8 * core + j)
+        first_sum[j] = first
+        second_sum[j] = second
+        return carry
+
+    lax.fori_loop(0, 8, for_own_rows, 0)
+    mate_outer = [pick(r[BLOCKS - 1 :], r[:1]) for r in mate]
+    mate_next = [pick(r[BLOCKS - 2 : BLOCKS - 1], r[1:2]) for r in mate]
+    mate_own = (mate_outer[0], jnp.exp2(mate_outer[1]), discount(mate_outer[2]), mate_outer[3])
+    mate_sums = added(
+        pair_sums(mate_own, *far_block(*mate_outer)), pair_sums(mate_own, *far_block(*mate_next))
+    )
+    outer_copy.wait_recv()
+    outer_turned[:, MAXQ:] = outer_in[...].T.astype(BF16)
+    outer_features[MAXQ:, :] = outer_in[...].astype(BF16)
+    mate_leaves = info_in[4]
+    outer_masks = [
+        leaf_mask(pick(leaves[:1], leaves[BLOCKS - 1 :])),
+        leaf_mask(pick(mate_leaves[BLOCKS - 1 :], mate_leaves[:1])),
+    ]
+    in_leaf[:, DEEP + MAXQ : ROWS] = outer_masks[0]
+    in_leaf[:, ROWS : ROWS + MAXQ] = outer_masks[1]
+
+    for slot in range(2):
+        remote(edge.at[0], halo.at[slot], halo_send.at[0], halo_recv.at[slot], plane(0, 0, 1)).wait_recv()
+    first_chip = (z == 0) & (y_lo == 0) & (x == 0) & (y_hi == 0)
+    last_chip = (z == depth - 1) & (y_lo == 1) & (x == 3) & (y_hi == 1)
+    top = iota((8, MAXQ), 0) == 0
+    was = jnp.where(top & first_chip, -1.0, halo[0])
+    will = jnp.where(top & last_chip, -1.0, halo[1])
+    near = pick(was, will)
+    far = pick(will, was)
+    outer = [pick(r[:1], r[BLOCKS - 1 :]) for r in own]
+    outer_sums = tuple(pick(a, b) for a, b in zip(sums[0], sums[BLOCKS - 1]))
+    ends = [
+        normalized(added(outer_sums, pair_sums(outer, *far_block(*[near[c : c + 1] for c in range(4)])))),
+        normalized(added(mate_sums, pair_sums(mate_own, *far_block(*[far[c : c + 1] for c in range(4)])))),
+    ]
+    out[0, pl.ds(core * (BLOCKS - 1), 1), :] = ends[0][0]
+    for k in range(2):
+        place = slice(MAXQ * k, MAXQ * (k + 1))
+        outer_weighted[:, place] = (outer_turned[:, place].astype(F32) * ends[k][1]).astype(BF16)
+    small = leaf_sums(
+        outer_masks, [e[0] for e in ends], [e[1] for e in ends], outer_features[...], outer_weighted[...]
+    )
+    for k in range(6):
+        end_sums[k] = small[k]
+
+    def outer_leaf(number):
+        mixed, diag, low = leaf_gram(
+            in_leaf[pl.ds(number, 1), DEEP + MAXQ : ROWS + MAXQ], outer_features[...], outer_weighted[...]
+        )
+        extra = stacked([end_sums[k, pl.ds(number, 1), :] for k in range(6)] + [diag])
+        first = jnp.concatenate(
+            [mixed[:64], extra, mixed[64:], jnp.zeros((8, HALF), F32)], axis=0
+        )
+        return first, low
 
     def p1x_copy(t):
         j, d = turn(t), lax.div(t, 2) + 1
@@ -472,11 +538,10 @@
 
     def for_own(t, carry):
         j = turn(t)
-        number = 8 * core + j
-        first, second = packed_leaf(number)
+        first, second = outer_leaf(8 * core + j)
         pair_copy(j).wait_recv()
-        first_sum[j] = first + pair_in[j, :144, :]
-        second_sum[j] = second + pair_in[j, 144:, :]
+        first_sum[j] = first_sum[j] + first + pair_in[j, :144, :]
+        second_sum[j] = second_sum[j] + second + pair_in[j, 144:, :]
 
         @pl.when(t < 6)
         def _():
@@ -621,6 +686,8 @@
         return carry
 
     lax.fori_loop(0, 8, sent, 0)
+    for copy in halos + [info_copy, outer_copy]:
+        copy.wait_send()
     for d in range(1, 4):
         p2x_copy(d).wait_send()
         p2y_copy(d).wait_send()
@@ -654,16 +721,17 @@
             pltpu.VMEM((F, EDGE), BF16),
             pltpu.VMEM((F, EDGE), BF16),
             pltpu.VMEM((EDGE, F), BF16),
-            pltpu.VMEM((LEAVES, ROWS), F32),
-            tile(6, LEAVES),
+            pltpu.VMEM((LEAVES, 2 * ROWS), F32),
+            tile(6, LEAVES), tile(6, LEAVES),
             tile(LEAVES, HALF), tile(LEAVES, 8), tile(LEAVES, HALF),
-            tile(2, 8), tile(8), tile(8),
+            tile(2, 8), tile(2, 8), tile(5, 8), tile(5, 8),
+            pltpu.VMEM((MAXQ, F), F32), pltpu.VMEM((MAXQ, F), F32),
             tile(8, LEAF_ROWS), tile(8, LEAF_ROWS),
             tile(8, 144), tile(8, 128), tile(3, 2, 144), tile(3, 2, 128),
             tile(4, 72), tile(4, 64), tile(3, 72), tile(3, 64),
             tile(8, 24), tile(7, 24), tile(24), tile(2, 8, 16), tile(2, 8, 8), tile(8),
             tile(LEAVES, 8),
-            dma((2,)), dma((2,)), dma((8,)), dma((8,)),
+            dma((2,)), dma((2,)), dma((2,)), dma((2,)), dma((8,)), dma((8,)),
             dma((8,)), dma((3, 2)), dma((8,)), dma((3, 2)),
             dma((3,)), dma((3,)), dma((3,)), dma((3,)),
             dma((7,)), dma((7,)), dma((8,)), dma((2, 8)), dma((8,)), dma((2, 8)),

time: 65.9 us -> 64.5 us (0.979)
  Pallas kernels: 63.8 us -> 62.4 us
    pallas_call x1, Pallas kernels: 63.8 us -> 62.4 us  [body(): pl.pallas_call(level_kernel, out_shape=jax.ShapeDtypeStruct((3, BLOCKS, M...]
where the time goes in v4:
time: 64.5 us; the launch traced here: 64.3 us
  Pallas kernels  62.4 us (97%)
  local copies, waits for them, and re-layouts  1.29 us (2%)
    pallas_call x1, Pallas kernels, body(): pl.pallas_call(level_kernel, out_shape=jax.ShapeDtypeStruct((3, BLOCKS, M...  62.4 us
    another operation x1, local copies, waits for them, and re-layouts, body(): return (out[0].reshape(ROWS), out[1].reshape(ROWS), out[2].reshape(ROWS))  1.29 us

profile of v4, /device:TPU:1, one launch (start us, length us, event | category | flops | bytes accessed | tf_op | source)
XLA Modules:
  0.0 64.3 jit_solution(1851121056940913219)
XLA Ops:
  0.6 62.4 %shard_map.85 = f32[3,8,128]{2,1,0:T(8,128)} custom-call(bf16[1024,256]{1,0:T(8,128)(2,1)} %features.1, f32[8,128]{1,0:T(8,128)} %bitcast.11, s32[8,128]{1,0:T(8,128)} %bitcast.12, s32[8,128]{1,0:T(8,128)} %bitcast.13, s32[8,128]{1,0:T(8,128)} %bitcast.14, s32[8,128]{1,0:T(8,128)} %bitcast.15), custom_call_target="tpu_custom_call" | custom-call | tf_op jit(solution)/shard_map/pallas_call | solution.py:714
  63.0 1.3 %slice_bitcast_fusion = (f32[1024]{0:T(1024)}, f32[1024]{0:T(1024)}, f32[1024]{0:T(1024)}) fusion(f32[3,8,128]{2,1,0:T(8,128)} %shard_map.85), kind=kLoop, calls=%fused_computation | loop fusion | bytes 24576 | tf_op jit(solution)/shard_map/reshape;squeeze | solution.py:742

commit v5 on v4

--- a/solution.py
+++ b/solution.py
@@ -198,6 +198,10 @@
     n = m.shape[0]
     lane = iota((8, n), 1)
     sub = iota((8, n), 0)
+    kept = jnp.where(iota((n, n), 0) == iota((n, n), 1), m, 0.0)
+    unit = lax.rsqrt(jnp.sum(kept, axis=0, keepdims=True))
+    unit = unit * lax.rsqrt(jnp.sum(kept, axis=1, keepdims=True))
+    m = m * unit
     for k in range(0, n, p):
         top = k // 8 * 8
         cols = [jnp.broadcast_to(m[:, k + b : k + b + 1], m.shape) for b in range(p)]
@@ -223,7 +227,7 @@
                     tile = jnp.where(sub == k - top + a, scaled[a], tile)
             tiles[t] = tile
         m = jnp.concatenate([tiles[t] for t in range(0, n, 8)], axis=0)
-    return m
+    return m * unit
 
 
 def solved(mixed, extra, low):

time: 64.5 us -> 64.6 us (level)
  no operation moved by 1% of the time
where the time goes in v5:
time: 64.6 us; the launch traced here: 64.5 us
  Pallas kernels  62.5 us (97%)
  local copies, waits for them, and re-layouts  1.29 us (2%)
    pallas_call x1, Pallas kernels, body(): pl.pallas_call(level_kernel, out_shape=jax.ShapeDtypeStruct((3, BLOCKS, M...  62.5 us
    another operation x1, local copies, waits for them, and re-layouts, body(): return (out[0].reshape(ROWS), out[1].reshape(ROWS), out[2].reshape(ROWS))  1.29 us

profile of v5, /device:TPU:1, one launch (start us, length us, event | category | flops | bytes accessed | tf_op | source)
XLA Modules:
  0.0 64.5 jit_solution(17861142949176503287)
XLA Ops:
  0.6 62.5 %shard_map.85 = f32[3,8,128]{2,1,0:T(8,128)} custom-call(bf16[1024,256]{1,0:T(8,128)(2,1)} %features.1, f32[8,128]{1,0:T(8,128)} %bitcast.11, s32[8,128]{1,0:T(8,128)} %bitcast.12, s32[8,128]{1,0:T(8,128)} %bitcast.13, s32[8,128]{1,0:T(8,128)} %bitcast.14, s32[8,128]{1,0:T(8,128)} %bitcast.15), custom_call_target="tpu_custom_call" | custom-call | tf_op jit(solution)/shard_map/pallas_call | solution.py:718
  63.2 1.3 %slice_bitcast_fusion = (f32[1024]{0:T(1024)}, f32[1024]{0:T(1024)}, f32[1024]{0:T(1024)}) fusion(f32[3,8,128]{2,1,0:T(8,128)} %shard_map.85), kind=kLoop, calls=%fused_computation | loop fusion | bytes 24576 | tf_op jit(solution)/shard_map/reshape;squeeze | solution.py:746
